TPU v7x, 32 devices: a whole 2x2x4 slice. The times are simulated.
32 devices in a mesh: tm: 16 (over z, y, x), mp: 2 (over core).
Axes of the slice: x: 2, y: 2, z: 4, core: 2. Of those that a mesh axis runs over, the one named last changes fastest.
Arguments:
- queries: bfloat16 [4096, 1536], P('tm', 'mp'), may hold values from -300 to 300
- upstream: bfloat16 [4096, 1536], P('tm', 'mp'), may hold values from -180 to 180
- bounds: int32 [4096, 2], P('tm'), may hold values from 0 to 12288, as said below
- frame_keys: bfloat16 [12288, 1536], P('tm', 'mp'), may hold values from -6 to 6
- frame_values: bfloat16 [12288, 1536], P('tm', 'mp'), may hold values from -6 to 6
- hidden_pre: bfloat16 [12288, 3072], P('tm', 'mp'), may hold values from -9 to 9
- expand_weight: bfloat16 [1536, 3072], P(None, 'mp'), may hold values from -0.15625 to 0.15625
- shrink_weight: bfloat16 [3072, 1536], P('mp'), may hold values from -0.109375 to 0.109375
- key_weight: bfloat16 [1536, 1536], P(None, 'mp'), may hold values from -0.15625 to 0.15625
- value_weight: bfloat16 [1536, 1536], P(None, 'mp'), may hold values from -0.15625 to 0.15625
- kernel_taps: bfloat16 [31, 1536], P(None, 'mp'), may hold values from -1.1953125 to 1.1953125
Outputs:
- frame_gradient: bfloat16 [12288, 1536], P('tm', 'mp')
- query_gradient: bfloat16 [4096, 1536], P('tm', 'mp')
Inputs may be any that keep to these rules, and one draw needn't show every extreme that they name: `bounds`: row t holds a token's start (column 0) and end (column 1). With s = t // 256: (s - 1) * 768 <= start < end <= (s + 2) * 768 and end - start <= 768; in every draw some token has start = (s - 1) * 768, some token has end = (s + 2) * 768, and some token has end - start = 768.
All inputs are finite; a program needn't handle non-finite values.
Results may differ from a plain program's by a relative error of at most 0.019.
Values may be sent and summed in bfloat16 or wider, within the bound.
A program may use at most 128 MiB of HBM per device.

v0:
```python
import math

import jax
import jax.numpy as jnp
from jax import lax
from jax.sharding import PartitionSpec as P

HD = 96
KERNEL = 31
HALF = 15


masked_fill = -1e30


def shifted(value, axis, by):
    peers = lax.axis_size(axis)
    pairs = [(i, i + by) for i in range(peers) if 0 <= i + by < peers]
    return lax.ppermute(value, axis, pairs)


def extended(value, sides, width):
    for axis, dim in sides:
        peers, length = (lax.axis_size(axis), value.shape[dim])
        up = [(i, (i + 1) % peers) for i in range(peers - 1)]
        down = [(j, i) for i, j in up]
        last = lax.slice_in_dim(value, length - width, length, axis=dim)
        first = lax.slice_in_dim(value, 0, width, axis=dim)
        before = lax.ppermute(last, axis, up)
        after = lax.ppermute(first, axis, down)
        value = jnp.concatenate([before, value, after], axis=dim)
    return value


def contract_last(left, right):
    return lax.dot_general(
        left, right, (((1,), (1,)), ((), ())), preferred_element_type=jnp.float32
    )


def contract_first(left, right):
    return lax.dot_general(
        left, right, (((0,), (0,)), ((), ())), preferred_element_type=jnp.float32
    )


def silu_slope(hidden_pre):
    logistic = jax.nn.sigmoid(hidden_pre)
    return logistic * (1.0 + hidden_pre * (1.0 - logistic))


def shards(
    queries,
    upstream,
    bounds,
    frame_keys,
    frame_values,
    hidden_pre,
    expand_weight,
    shrink_weight,
    key_weight,
    value_weight,
    kernel_taps,
):
    frame_rows = frame_keys.shape[0]
    width_dev = queries.shape[1]
    heads_dev = width_dev // HD
    score_scale = 1.0 / math.sqrt(HD)
    shard_index = lax.axis_index("tm")
    own_positions = shard_index * frame_rows + jnp.arange(frame_rows, dtype=jnp.int32)
    visitors = {}
    for offset in (-1, 0, 1):
        if offset == 0:
            visitors[offset] = (queries, upstream, bounds)
        else:
            visitors[offset] = shifted((queries, upstream, bounds), "tm", -offset)
    saved = {}
    masks = {}
    partials = {}
    for offset in (-1, 0, 1):
        guest = visitors[offset]
        inside = (own_positions[None, :] >= guest[2][:, 0:1]) & (
            own_positions[None, :] < guest[2][:, 1:2]
        )
        masks[offset] = inside
        maxima, totals, weighted = ([], [], [])
        for head_index in range(heads_dev):
            columns = slice(head_index * HD, (head_index + 1) * HD)
            scores = contract_last(guest[0][:, columns], frame_keys[:, columns]) * score_scale
            slopes = contract_last(guest[1][:, columns], frame_values[:, columns])
            row_max = jnp.max(jnp.where(inside, scores, masked_fill), 1)
            expos = jnp.where(inside, jnp.exp(scores - row_max[:, None]), 0.0)
            maxima.append(row_max)
            totals.append(jnp.sum(expos, 1))
            weighted.append(jnp.sum(expos * slopes, 1))
            saved[offset, head_index] = (scores, slopes)
        partials[offset] = (jnp.stack(maxima, 1), jnp.stack(totals, 1), jnp.stack(weighted, 1))
    collected = [partials[0]]
    for offset in (-1, 1):
        collected.append(shifted(partials[offset], "tm", offset))
    peak = jnp.maximum(jnp.maximum(collected[0][0], collected[1][0]), collected[2][0])
    row_sum = jnp.zeros_like(peak)
    weighted_sum = jnp.zeros_like(peak)
    for stats in collected:
        factor = jnp.exp(stats[0] - peak)
        row_sum = row_sum + stats[1] * factor
        weighted_sum = weighted_sum + stats[2] * factor
    log_total = peak + jnp.log(row_sum)
    row_delta = weighted_sum / row_sum
    norms = {0: (log_total, row_delta)}
    for offset in (-1, 1):
        norms[offset] = shifted((log_total, row_delta), "tm", -offset)
    key_sums = [jnp.zeros((frame_rows, HD), jnp.float32) for head_index in range(heads_dev)]
    value_sums = [jnp.zeros((frame_rows, HD), jnp.float32) for head_index in range(heads_dev)]
    query_terms = {}
    for offset in (-1, 0, 1):
        guest = visitors[offset]
        inside = masks[offset]
        head_terms = []
        for head_index in range(heads_dev):
            columns = slice(head_index * HD, (head_index + 1) * HD)
            scores, slopes = saved[offset, head_index]
            probabilities = jnp.where(
                inside, jnp.exp(scores - norms[offset][0][:, head_index : head_index + 1]), 0.0
            )
            score_gradient = (
                probabilities
                * (slopes - norms[offset][1][:, head_index : head_index + 1])
                * score_scale
            ).astype(jnp.bfloat16)
            head_terms.append(
                jnp.dot(score_gradient, frame_keys[:, columns], preferred_element_type=jnp.float32)
            )
            key_sums[head_index] = key_sums[head_index] + contract_first(
                score_gradient, guest[0][:, columns]
            )
            value_sums[head_index] = value_sums[head_index] + contract_first(
                probabilities.astype(jnp.bfloat16), guest[1][:, columns]
            )
        query_terms[offset] = jnp.concatenate(head_terms, 1)
    query_total = query_terms[0]
    for offset in (-1, 1):
        query_total = query_total + shifted(
            query_terms[offset].astype(jnp.bfloat16), "tm", offset
        ).astype(jnp.float32)
    query_gradient = query_total.astype(jnp.bfloat16)
    key_gradient = jnp.concatenate(key_sums, 1)
    value_gradient = jnp.concatenate(value_sums, 1)
    key_low = key_gradient.astype(jnp.bfloat16)
    value_low = value_gradient.astype(jnp.bfloat16)
    partial_value = contract_last(key_low, key_weight) + contract_last(value_low, value_weight)
    encoder_sum = lax.psum(partial_value.astype(jnp.bfloat16), "mp").astype(jnp.float32)
    encoder_low = encoder_sum.astype(jnp.bfloat16)
    act_gradient = 0.5 * contract_last(encoder_low, shrink_weight)
    pre_gradient = (act_gradient * silu_slope(hidden_pre.astype(jnp.float32))).astype(jnp.bfloat16)
    hidden_part = contract_last(pre_gradient, expand_weight)
    hidden_back = lax.psum_scatter(
        hidden_part.astype(jnp.bfloat16), "mp", scatter_dimension=1, tiled=True
    ).astype(jnp.float32)
    column_start = lax.axis_index("mp") * width_dev
    hidden_gradient = (
        lax.dynamic_slice_in_dim(encoder_sum, column_start, width_dev, 1) + hidden_back
    ).astype(jnp.bfloat16)
    padded = extended(hidden_gradient, (("tm", 0),), HALF)
    weights = kernel_taps.astype(jnp.float32)
    result = hidden_gradient.astype(jnp.float32)
    for tap_index in range(KERNEL):
        lower_row = 2 * HALF - tap_index
        result = result + weights[tap_index] * padded[lower_row : lower_row + frame_rows].astype(
            jnp.float32
        )
    return (result.astype(jnp.bfloat16), query_gradient)


def solution(mesh):
    placed = (
        P("tm", "mp"),
        P("tm", "mp"),
        P("tm", None),
        P("tm", "mp"),
        P("tm", "mp"),
        P("tm", "mp"),
        P(None, "mp"),
        P("mp", None),
        P(None, "mp"),
        P(None, "mp"),
        P(None, "mp"),
    )
    return jax.shard_map(
        shards,
        mesh=mesh,
        in_specs=placed,
        out_specs=(P("tm", "mp"), P("tm", "mp")),
        check_vma=False,
    )
```

profile of v0, /device:TPU:8, one launch (start us, length us, event | category | flops | bytes accessed | tf_op | source)
XLA Modules:
  0.0 376.3 jit_solution(7947670596207128647)
XLA Ops:
  7.2 4.5 %collective-permute-start.4 = (bf16[256,768]{1,0:T(8,128)(2,1)}, bf16[256,768]{1,0:T(8,128)(2,1)}, u32[]{:S(2)}, u32[]{:S(2)}) collective-permute-start(bf16[256,768]{1,0:T(8,128)(2,1)} %param.11), channel_id=1, source_target_pairs={{2,0},{4,2},{6,4},{8,6},{10,8},{12,10},{14,12},{16,14},{18,16},{20... | collective-permute-start | bytes 1179656 | tf_op jit(solution)/shard_map/ppermute | solution.py:19
  13.7 5.7 %collective-permute-start.3 = (s32[256,2]{0,1:T(2,128)}, s32[256,2]{0,1:T(2,128)S(1)}, u32[]{:S(2)}, u32[]{:S(2)}) collective-permute-start(s32[256,2]{0,1:T(2,128)} %param.13), channel_id=1, source_target_pairs={{2,0},{4,2},{6,4},{8,6},{10,8},{12,10},{14,12},{16,14},{18,16},{20... | collective-permute-start | bytes 6152 | tf_op jit(solution)/shard_map/ppermute | solution.py:19
  21.4 5.7 %collective-permute-start.11 = (bf16[256,768]{1,0:T(8,128)(2,1)}, bf16[256,768]{1,0:T(8,128)(2,1)}, u32[]{:S(2)}, u32[]{:S(2)}) collective-permute-start(bf16[256,768]{1,0:T(8,128)(2,1)} %param.12), channel_id=1, source_target_pairs={{2,0},{4,2},{6,4},{8,6},{10,8},{12,10},{14,12},{16,14},{18,16},{20... | collective-permute-start | bytes 1179656 | tf_op jit(solution)/shard_map/ppermute | solution.py:19
  30.0 2.3 convolution_multiply_fusion.16
  32.3 2.5 convolution_multiply_fusion.17
  46.5 2.6 fusion.284
  55.8 4.9 %fusion.115 = (f32[256]{0:T(256)}, f32[256]{0:T(256)}, f32[256]{0:T(256)}, f32[256]{0:T(256)}, f32[256]{0:T(256)}, /*index=5*/f32[256]{0:T(256)}, f32[256]{0:T(2...) fusion(f32[256,768]{1,0:T(8,128)S(1)} %get-tuple-element.227, ...), kind=kOutput, calls=%fused_computation.357 | convolution fusion | flops 44037120 | bytes 9721856 | tf_op jit(solution)/shard_map/dot_general | solution.py:36
  80.6 3.9 %fusion.131 = (f32[256]{0:T(256)}, f32[256]{0:T(256)}, f32[256]{0:T(256)}, f32[256]{0:T(256)}, f32[256]{0:T(256)}, /*index=5*/f32[256]{0:T(256)}, f32[256]{0:T(2...) fusion(f32[256,768]{1,0:T(8,128)S(1)} %convolution_multiply_fusion, ...), kind=kOutput, calls=%fused_computation.373 | convolution fusion | flops 42661376 | bytes 8144896 | tf_op jit(solution)/shard_map/dot_general | solution.py:36
  85.8 3.6 fusion.113
  91.1 2.8 fusion.123
  96.0 3.4 fusion.122
  100.7 6.0 %collective-permute-start.10 = (f32[256,8]{0,1:T(8,128)}, f32[256,8]{0,1:T(8,128)}, u32[]{:S(2)}, u32[]{:S(2)}) collective-permute-start(f32[256,8]{0,1:T(8,128)} %stack.314), channel_id=1, source_target_pairs={{2,0},{4,2},{6,4},{8,6},{10,8},{12,10},{14,12},{16,14},{18,16},{20... | collective-permute-start | bytes 24584 | tf_op jit(solution)/shard_map/ppermute | solution.py:19
  113.0 4.0 %fusion.130 = (f32[256]{0:T(256)}, f32[256]{0:T(256)}, f32[256]{0:T(256)}, f32[256]{0:T(256)}, f32[256]{0:T(256)}, /*index=5*/f32[256]{0:T(256)}, f32[256]{0:T(2...) fusion(f32[256,768]{1,0:T(8,128)S(1)} %copy-done.52, f32[256]{0:T(256)} %get-tuple-element.122, ...), kind=kOutput, calls=%fused_computation.372 | convolution fusion | flops 43251200 | bytes 8146944 | tf_op jit(solution)/shard_map/dot_general | solution.py:36
  124.8 5.7 %collective-permute-start.2 = (f32[256,8]{0,1:T(8,128)}, f32[256,8]{0,1:T(8,128)}, u32[]{:S(2)}, u32[]{:S(2)}) collective-permute-start(f32[256,8]{0,1:T(8,128)} %stack.260), channel_id=1, source_target_pairs={{2,0},{4,2},{6,4},{8,6},{10,8},{12,10},{14,12},{16,14},{18,16},{20... | collective-permute-start | bytes 24584 | tf_op jit(solution)/shard_map/ppermute | solution.py:19
  131.9 3.9 %collective-permute-start.6 = (f32[256,8]{0,1:T(8,128)}, f32[256,8]{0,1:T(8,128)}, u32[]{:S(2)}, u32[]{:S(2)}) collective-permute-start(f32[256,8]{0,1:T(8,128)} %stack.287), channel_id=1, source_target_pairs={{2,0},{4,2},{6,4},{8,6},{10,8},{12,10},{14,12},{16,14},{18,16},{20... | collective-permute-start | bytes 24584 | tf_op jit(solution)/shard_map/ppermute | solution.py:19
  139.0 5.8 %fusion.114 = (f32[256]{0:T(256)}, f32[256]{0:T(256)}, f32[256]{0:T(256)}, f32[256]{0:T(256)}, f32[256]{0:T(256)}, /*index=5*/f32[256]{0:T(256)}, f32[256]{0:T(2...) fusion(f32[256,768]{1,0:T(8,128)} %convolution_multiply_fusion.16, ...), kind=kOutput, calls=%fused_computation.356 | convolution fusion | flops 43251200 | bytes 8146944 | tf_op jit(solution)/shard_map/dot_general | solution.py:36
  151.8 3.9 %collective-permute-start.13 = (f32[256,8]{0,1:T(8,128)S(1)}, f32[256,8]{0,1:T(8,128)S(1)}, u32[]{:S(2)}, u32[]{:S(2)}) collective-permute-start(f32[256,8]{0,1:T(8,128)S(1)} %get-tuple-element.148), channel_id=1, source_target_pairs={{0,2},{2,4},{4,6},{6,8},{8,10},{10,12},{12,14},{14,16},{16,18},{18... | collective-permute-start | bytes 24584 | tf_op jit(solution)/shard_map/ppermute | solution.py:19
  155.7 3.7 collective-permute-start.14
  159.4 3.8 %collective-permute-start.15 = (f32[256,8]{0,1:T(8,128)S(1)}, f32[256,8]{0,1:T(8,128)S(1)}, u32[]{:S(2)}, u32[]{:S(2)}) collective-permute-start(f32[256,8]{0,1:T(8,128)S(1)} %get-tuple-element.148), channel_id=1, source_target_pairs={{2,0},{4,2},{6,4},{8,6},{10,8},{12,10},{14,12},{16,14},{18,16},{20... | collective-permute-start | bytes 24584 | tf_op jit(solution)/shard_map/ppermute | solution.py:19
  163.3 2.5 fusion.158
  165.8 2.5 fusion.163
  220.4 3.7 concatenate.54
  224.3 5.5 %fusion.488 = f32[768,1536]{1,0:T(8,128)} fusion(bf16[768,768]{1,0:T(8,128)(2,1)} %concatenate.54, bf16[1536,768]{1,0:T(8,128)(2,1)S(1)} %copy-done), kind=kOutput, calls=%fused_computation.745 | convolution fusion | flops 1811939328 | bytes 8257536 | tf_op jit(solution)/shard_map/dot_general | solution.py:36
  251.6 2.2 concatenate.55
  253.8 6.5 %add_convert_fusion = bf16[768,1536]{1,0:T(8,128)(2,1)} fusion(f32[768,1536]{1,0:T(8,128)} %fusion.488, bf16[768,768]{1,0:T(8,128)(2,1)S(1)} %concatenate.55, bf16[1536,768]{1,0:T(8,128)(2,1)} %param.20), kind=kOutput, calls=%fused_computation.37 | convolution fusion | flops 1814298624 | bytes 10616832 | tf_op jit(solution)/shard_map/dot_general | solution.py:36
  264.3 19.0 %all-reduce.2.cloned.1.call-done = bf16[768,1536]{1,0:T(8,128)(2,1)} async-done(((bf16[768,1536]{1,0:T(8,128)(2,1)}), bf16[768,1536]{1,0:T(8,128)(2,1)}) %all-reduce.2.cloned.1.call-update) | async-done | bytes 2359312 | tf_op jit(solution)/shard_map/psum | solution.py:152
  283.3 14.1 %convolution_convert_fusion = bf16[768,1536]{1,0:T(8,128)(2,1)} fusion(bf16[1536,1536]{1,0:T(8,128)(2,1)} %param.17, bf16[768,1536]{1,0:T(8,128)(2,1)} %param.16, bf16[768,1536]{1,0:T(8,128)(2,1)} %all-reduce.2.cloned.1.call-done, bf16[1536,1536]{1,0:T(8,128)(2,1)} %param.18), kind=kOutput, calls=%fused_computation.38 | convolution fusion | flops 7261913088 | bytes 16515072 | tf_op jit(solution)/shard_map/dot_general | solution.py:36
  311.9 4.4 %collective-permute-start.18 = (bf16[256,768]{0,1:T(8,128)(2,1)}, bf16[256,768]{0,1:T(8,128)(2,1)}, u32[]{:S(2)}, u32[]{:S(2)}) collective-permute-start(bf16[256,768]{0,1:T(8,128)(2,1)} %fusion.100), channel_id=1, source_target_pairs={{2,0},{4,2},{6,4},{8,6},{10,8},{12,10},{14,12},{16,14},{18,16},{20... | collective-permute-start | bytes 1179656 | tf_op jit(solution)/shard_map/ppermute | solution.py:19
  328.9 5.7 %collective-permute-start.16 = (bf16[15,768]{1,0:T(8,128)(2,1)}, bf16[15,768]{1,0:T(8,128)(2,1)}, u32[]{:S(2)}, u32[]{:S(2)}) collective-permute-start(bf16[15,768]{1,0:T(8,128)(2,1)} %get-tuple-element.145), channel_id=1, source_target_pairs={{2,0},{4,2},{6,4},{8,6},{10,8},{12,10},{14,12},{16,14},{18,16},{20... | collective-permute-start | bytes 69128 | tf_op jit(solution)/shard_map/ppermute | solution.py:30
  334.7 2.3 collective-permute-start.17
  337.0 2.6 collective-permute-done.19
  343.7 25.4 %add_convert_fusion.1 = bf16[768,768]{1,0:T(8,128)(2,1)} fusion(bf16[768,768]{1,0:T(8,128)(2,1)S(1)} %add_convert_fusion.2, bf16[15,768]{1,0:T(8,128)(2,1)} %collective-permute-done.17, bf16[15,768]{1,0:T(8,128)(2,1)} %collective-permute-done.16, f32[768]{0:T(1024)S(1)} %get-tuple-element.55, f32[768]{0:T(1024)S(1)} %get-tuple-element.56, ...), kind=kLoop, calls=%fused_computation.66 | loop fusion | flops 108527616 | bytes 2500608 | tf_op jit(solution)/shard_map/convert_element_type | solution.py:172
  (638 shorter events, 183.5 us)
Async XLA Ops:
  7.2 217.0 %copy-start = (bf16[1536,768]{1,0:T(8,128)(2,1)S(1)}, bf16[1536,768]{1,0:T(8,128)(2,1)}, u32[]{:S(2)}) copy-start(bf16[1536,768]{1,0:T(8,128)(2,1)} %param.19) | copy-start | bytes 7077892
  7.2 27.6 %copy-start.2 = (bf16[768,768]{1,0:T(8,128)(2,1)S(1)}, bf16[768,768]{1,0:T(8,128)(2,1)}, u32[]{:S(2)}) copy-start(bf16[768,768]{1,0:T(8,128)(2,1)} %param.14) | copy-start | bytes 3538948
  7.2 276.1 %all-reduce.2.cloned.1.call-start = ((), (), s32[]{:S(2)}) async-start(), calls=%async_computation.1 | async-start | bytes 4718592 | tf_op jit(solution)/shard_map/psum | solution.py:152
  7.2 27.5 %copy-start.155 = (bf16[256,768]{1,0:T(8,128)(2,1)S(1)}, bf16[256,768]{1,0:T(8,128)(2,1)}, u32[]{:S(2)}) copy-start(bf16[256,768]{1,0:T(8,128)(2,1)} %param.11) | copy-start | bytes 1179652
  7.2 46.0 %collective-permute-start.4 = (bf16[256,768]{1,0:T(8,128)(2,1)}, bf16[256,768]{1,0:T(8,128)(2,1)}, u32[]{:S(2)}, u32[]{:S(2)}) collective-permute-start(bf16[256,768]{1,0:T(8,128)(2,1)} %param.11), channel_id=1, source_target_pairs={{2,0},{4,2},{6,4},{8,6},{10,8},{12,10},{14,12},{16,14},{18,16},{20... | collective-permute-start | bytes 1179656 | tf_op jit(solution)/shard_map/ppermute | solution.py:19
  11.8 56.9 %collective-permute-start.1 = (bf16[256,768]{1,0:T(8,128)(2,1)}, bf16[256,768]{1,0:T(8,128)(2,1)}, u32[]{:S(2)}, u32[]{:S(2)}) collective-permute-start(bf16[256,768]{1,0:T(8,128)(2,1)} %param.11), channel_id=1, source_target_pairs={{0,2},{2,4},{4,6},{6,8},{8,10},{10,12},{12,14},{14,16},{16,18},{18... | collective-permute-start | bytes 1179656 | tf_op jit(solution)/shard_map/ppermute | solution.py:19
  13.7 35.4 %collective-permute-start.3 = (s32[256,2]{0,1:T(2,128)}, s32[256,2]{0,1:T(2,128)S(1)}, u32[]{:S(2)}, u32[]{:S(2)}) collective-permute-start(s32[256,2]{0,1:T(2,128)} %param.13), channel_id=1, source_target_pairs={{2,0},{4,2},{6,4},{8,6},{10,8},{12,10},{14,12},{16,14},{18,16},{20... | collective-permute-start | bytes 6152 | tf_op jit(solution)/shard_map/ppermute | solution.py:19
  19.4 33.1 %collective-permute-start = (s32[256,2]{0,1:T(2,128)}, s32[256,2]{0,1:T(2,128)}, u32[]{:S(2)}, u32[]{:S(2)}) collective-permute-start(s32[256,2]{0,1:T(2,128)} %param.13), channel_id=1, source_target_pairs={{0,2},{2,4},{4,6},{6,8},{8,10},{10,12},{12,14},{14,16},{16,18},{18... | collective-permute-start | bytes 6152 | tf_op jit(solution)/shard_map/ppermute | solution.py:19
  21.4 49.8 %collective-permute-start.11 = (bf16[256,768]{1,0:T(8,128)(2,1)}, bf16[256,768]{1,0:T(8,128)(2,1)}, u32[]{:S(2)}, u32[]{:S(2)}) collective-permute-start(bf16[256,768]{1,0:T(8,128)(2,1)} %param.12), channel_id=1, source_target_pairs={{2,0},{4,2},{6,4},{8,6},{10,8},{12,10},{14,12},{16,14},{18,16},{20... | collective-permute-start | bytes 1179656 | tf_op jit(solution)/shard_map/ppermute | solution.py:19
  49.7 39.8 %collective-permute-start.9 = (bf16[256,768]{1,0:T(8,128)(2,1)}, bf16[256,768]{1,0:T(8,128)(2,1)S(1)}, u32[]{:S(2)}, u32[]{:S(2)}) collective-permute-start(bf16[256,768]{1,0:T(8,128)(2,1)} %param.12), channel_id=1, source_target_pairs={{0,2},{2,4},{4,6},{6,8},{8,10},{10,12},{12,14},{14,16},{16,18},{18... | collective-permute-start | bytes 1179656 | tf_op jit(solution)/shard_map/ppermute | solution.py:19
  52.5 33.2 %copy-start.177 = (s32[256,1]{0,1:T(1,128)}, s32[256,1]{0,1:T(1,128)S(1)}, u32[]{:S(2)}) copy-start(s32[256,1]{0,1:T(1,128)S(1)} %get-tuple-element.224) | copy-start | bytes 3076
  54.5 26.0 %copy-start.23 = (f32[256,768]{1,0:T(8,128)}, f32[256,768]{1,0:T(8,128)S(1)}, u32[]{:S(2)}) copy-start(f32[256,768]{1,0:T(8,128)S(1)} %convolution_multiply_fusion) | copy-start | bytes 2359300
  100.7 36.4 %collective-permute-start.10 = (f32[256,8]{0,1:T(8,128)}, f32[256,8]{0,1:T(8,128)}, u32[]{:S(2)}, u32[]{:S(2)}) collective-permute-start(f32[256,8]{0,1:T(8,128)} %stack.314), channel_id=1, source_target_pairs={{2,0},{4,2},{6,4},{8,6},{10,8},{12,10},{14,12},{16,14},{18,16},{20... | collective-permute-start | bytes 24584 | tf_op jit(solution)/shard_map/ppermute | solution.py:19
  118.4 30.4 %collective-permute-start.12 = (f32[256,8]{0,1:T(8,128)}, f32[256,8]{0,1:T(8,128)}, u32[]{:S(2)}, u32[]{:S(2)}) collective-permute-start(f32[256,8]{0,1:T(8,128)} %stack.323), channel_id=1, source_target_pairs={{0,2},{2,4},{4,6},{6,8},{8,10},{10,12},{12,14},{14,16},{16,18},{18... | collective-permute-start | bytes 24584 | tf_op jit(solution)/shard_map/ppermute | solution.py:19
  121.6 27.2 %collective-permute-start.5 = (f32[256,8]{0,1:T(8,128)}, f32[256,8]{0,1:T(8,128)}, u32[]{:S(2)}, u32[]{:S(2)}) collective-permute-start(f32[256,8]{0,1:T(8,128)} %stack.269), channel_id=1, source_target_pairs={{0,2},{2,4},{4,6},{6,8},{8,10},{10,12},{12,14},{14,16},{16,18},{18... | collective-permute-start | bytes 24584 | tf_op jit(solution)/shard_map/ppermute | solution.py:19
  124.8 23.9 %collective-permute-start.2 = (f32[256,8]{0,1:T(8,128)}, f32[256,8]{0,1:T(8,128)}, u32[]{:S(2)}, u32[]{:S(2)}) collective-permute-start(f32[256,8]{0,1:T(8,128)} %stack.260), channel_id=1, source_target_pairs={{2,0},{4,2},{6,4},{8,6},{10,8},{12,10},{14,12},{16,14},{18,16},{20... | collective-permute-start | bytes 24584 | tf_op jit(solution)/shard_map/ppermute | solution.py:19
  131.9 16.9 %collective-permute-start.6 = (f32[256,8]{0,1:T(8,128)}, f32[256,8]{0,1:T(8,128)}, u32[]{:S(2)}, u32[]{:S(2)}) collective-permute-start(f32[256,8]{0,1:T(8,128)} %stack.287), channel_id=1, source_target_pairs={{2,0},{4,2},{6,4},{8,6},{10,8},{12,10},{14,12},{16,14},{18,16},{20... | collective-permute-start | bytes 24584 | tf_op jit(solution)/shard_map/ppermute | solution.py:19
  137.1 11.7 %collective-permute-start.7 = (f32[256,8]{0,1:T(8,128)}, f32[256,8]{0,1:T(8,128)}, u32[]{:S(2)}, u32[]{:S(2)}) collective-permute-start(f32[256,8]{0,1:T(8,128)} %stack.296), channel_id=1, source_target_pairs={{0,2},{2,4},{4,6},{6,8},{8,10},{10,12},{12,14},{14,16},{16,18},{18... | collective-permute-start | bytes 24584 | tf_op jit(solution)/shard_map/ppermute | solution.py:19
  149.7 33.5 %collective-permute-start.8 = (f32[256,8]{0,1:T(8,128)S(1)}, f32[256,8]{0,1:T(8,128)S(1)}, u32[]{:S(2)}, u32[]{:S(2)}) collective-permute-start(f32[256,8]{0,1:T(8,128)S(1)} %get-tuple-element.147), channel_id=1, source_target_pairs={{0,2},{2,4},{4,6},{6,8},{8,10},{10,12},{12,14},{14,16},{16,18},{18... | collective-permute-start | bytes 24584 | tf_op jit(solution)/shard_map/ppermute | solution.py:19
  151.8 31.5 %collective-permute-start.13 = (f32[256,8]{0,1:T(8,128)S(1)}, f32[256,8]{0,1:T(8,128)S(1)}, u32[]{:S(2)}, u32[]{:S(2)}) collective-permute-start(f32[256,8]{0,1:T(8,128)S(1)} %get-tuple-element.148), channel_id=1, source_target_pairs={{0,2},{2,4},{4,6},{6,8},{8,10},{10,12},{12,14},{14,16},{16,18},{18... | collective-permute-start | bytes 24584 | tf_op jit(solution)/shard_map/ppermute | solution.py:19
  155.7 29.8 %collective-permute-start.14 = (f32[256,8]{0,1:T(8,128)S(1)}, f32[256,8]{0,1:T(8,128)S(1)}, u32[]{:S(2)}, u32[]{:S(2)}) collective-permute-start(f32[256,8]{0,1:T(8,128)S(1)} %get-tuple-element.147), channel_id=1, source_target_pairs={{2,0},{4,2},{6,4},{8,6},{10,8},{12,10},{14,12},{16,14},{18,16},{20... | collective-permute-start | bytes 24584 | tf_op jit(solution)/shard_map/ppermute | solution.py:19
  159.4 26.2 %collective-permute-start.15 = (f32[256,8]{0,1:T(8,128)S(1)}, f32[256,8]{0,1:T(8,128)S(1)}, u32[]{:S(2)}, u32[]{:S(2)}) collective-permute-start(f32[256,8]{0,1:T(8,128)S(1)} %get-tuple-element.148), channel_id=1, source_target_pairs={{2,0},{4,2},{6,4},{8,6},{10,8},{12,10},{14,12},{16,14},{18,16},{20... | collective-permute-start | bytes 24584 | tf_op jit(solution)/shard_map/ppermute | solution.py:19
  185.5 25.6 %copy-start.96 = (bf16[256,768]{1,0:T(8,128)(2,1)}, bf16[256,768]{1,0:T(8,128)(2,1)S(1)}, u32[]{:S(2)}) copy-start(bf16[256,768]{1,0:T(8,128)(2,1)S(1)} %get-tuple-element.209) | copy-start | bytes 1179652
  185.5 29.3 %copy-start.98 = (bf16[256,768]{1,0:T(8,128)(2,1)}, bf16[256,768]{1,0:T(8,128)(2,1)S(1)}, u32[]{:S(2)}) copy-start(bf16[256,768]{1,0:T(8,128)(2,1)S(1)} %get-tuple-element.210) | copy-start | bytes 1179652
  185.5 31.2 %copy-start.100 = (bf16[256,768]{1,0:T(8,128)(2,1)}, bf16[256,768]{1,0:T(8,128)(2,1)S(1)}, u32[]{:S(2)}) copy-start(bf16[256,768]{1,0:T(8,128)(2,1)S(1)} %get-tuple-element.211) | copy-start | bytes 1179652
  185.5 33.1 %copy-start.102 = (bf16[256,768]{1,0:T(8,128)(2,1)}, bf16[256,768]{1,0:T(8,128)(2,1)S(1)}, u32[]{:S(2)}) copy-start(bf16[256,768]{1,0:T(8,128)(2,1)S(1)} %get-tuple-element.212) | copy-start | bytes 1179652
  260.4 66.0 %reduce-scatter.2.cloned.1.call-start = ((), (), s32[]{:S(2)}) async-start(), calls=%async_computation.2 | async-start | bytes 3538944 | tf_op jit(solution)/shard_map/reduce_scatter | solution.py:157
  311.9 25.1 %collective-permute-start.18 = (bf16[256,768]{0,1:T(8,128)(2,1)}, bf16[256,768]{0,1:T(8,128)(2,1)}, u32[]{:S(2)}, u32[]{:S(2)}) collective-permute-start(bf16[256,768]{0,1:T(8,128)(2,1)} %fusion.100), channel_id=1, source_target_pairs={{2,0},{4,2},{6,4},{8,6},{10,8},{12,10},{14,12},{16,14},{18,16},{20... | collective-permute-start | bytes 1179656 | tf_op jit(solution)/shard_map/ppermute | solution.py:19
  324.5 15.1 %collective-permute-start.19 = (bf16[256,768]{0,1:T(8,128)(2,1)}, bf16[256,768]{0,1:T(8,128)(2,1)}, u32[]{:S(2)}, u32[]{:S(2)}) collective-permute-start(bf16[256,768]{0,1:T(8,128)(2,1)} %fusion.92), channel_id=1, source_target_pairs={{0,2},{2,4},{4,6},{6,8},{8,10},{10,12},{12,14},{14,16},{16,18},{18... | collective-permute-start | bytes 1179656 | tf_op jit(solution)/shard_map/ppermute | solution.py:19
  328.9 14.8 %collective-permute-start.16 = (bf16[15,768]{1,0:T(8,128)(2,1)}, bf16[15,768]{1,0:T(8,128)(2,1)}, u32[]{:S(2)}, u32[]{:S(2)}) collective-permute-start(bf16[15,768]{1,0:T(8,128)(2,1)} %get-tuple-element.145), channel_id=1, source_target_pairs={{2,0},{4,2},{6,4},{8,6},{10,8},{12,10},{14,12},{16,14},{18,16},{20... | collective-permute-start | bytes 69128 | tf_op jit(solution)/shard_map/ppermute | solution.py:30
  334.7 34.5 %copy-start.1 = (bf16[1536,768]{1,0:T(8,128)(2,1)S(1)}, bf16[1536,768]{1,0:T(8,128)(2,1)}, u32[]{:S(2)}) copy-start(bf16[1536,768]{1,0:T(8,128)(2,1)} %param.19) | copy-start | bytes 7077892
  334.7 9.0 %collective-permute-start.17 = (bf16[15,768]{1,0:T(8,128)(2,1)}, bf16[15,768]{1,0:T(8,128)(2,1)}, u32[]{:S(2)}, u32[]{:S(2)}) collective-permute-start(bf16[15,768]{1,0:T(8,128)(2,1)} %get-tuple-element.146), channel_id=1, source_target_pairs={{0,2},{2,4},{4,6},{6,8},{8,10},{10,12},{12,14},{14,16},{16,18},{18... | collective-permute-start | bytes 69128 | tf_op jit(solution)/shard_map/ppermute | solution.py:29
  (223 other events, 1479.4 us)
Sparse Core Ops, SparseCore 0:
  260.5 22.7 all-reduce.1
  297.6 11.2 reduce-scatter.1
where the time goes:
time: 383 us; the launch traced here: 376 us
  matrix products  193 us (50%)
  starting transfers between devices  71.3 us (19%)
  other arithmetic  37.6 us (10%)
  local copies, waits for them, and re-layouts  34.9 us (9%)
  waiting for transfers between devices  21.7 us (6%)
  between operations  17.5 us (5%)
    dot_general x51, matrix products, contract_last(): lax.dot_general(left, right, (((1,), (1,)), ((), ())), preferred_element_...  108 us
    ppermute x18, starting transfers between devices, shifted(): return lax.ppermute(value, axis, pairs)  63 us
    dot_general x48, matrix products, contract_first(): lax.dot_general(left, right, (((0,), (0,)), ((), ())), preferred_element_...  61.7 us
    convert_element_type x1, other arithmetic, shards(): return (result.astype(jnp.bfloat16), query_gradient)  25.4 us
    dot_general x24, matrix products, shards(): jnp.dot(score_gradient, frame_keys[:, columns], preferred_element_type=jn...  23.2 us
    psum x1, waiting for transfers between devices, shards(): lax.psum(partial_value.astype(jnp.bfloat16), 'mp').astype(jnp.float32)  19 us
    unnamed x467, local copies, waits for them, and re-layouts  12.7 us
  transfers between devices with their start and end apart: 22, of which 2 were waited for; matrix products, arithmetic and copies ran while one was open for 36% of the time, Pallas kernels for 0%

commit v1 on v0

v1 whole, which is shorter than its diff:
```python
import functools
import math

import jax
import jax.numpy as jnp
from jax import lax
from jax.experimental import pallas as pl
from jax.experimental.pallas import tpu as pltpu
from jax.sharding import PartitionSpec as P

HD = 96
KERNEL = 31
HALF = 15
LANES = 128
HALO = 16
masked_fill = -1e30
VMEM = pl.BlockSpec(memory_space=pltpu.VMEM)


def shifted(value, axis, by):
    peers = lax.axis_size(axis)
    pairs = [(i, i + by) for i in range(peers) if 0 <= i + by < peers]
    return lax.ppermute(value, axis, pairs)


def contract_last(left, right):
    return lax.dot_general(
        left, right, (((1,), (1,)), ((), ())), preferred_element_type=jnp.float32
    )


def mm(left, right):
    return jnp.dot(left, right, preferred_element_type=jnp.float32)


def silu_slope(hidden_pre):
    logistic = jax.nn.sigmoid(hidden_pre)
    return logistic * (1.0 + hidden_pre * (1.0 - logistic))


def window_of(width):
    return min(2 * LANES, width)


def window_start(pair):
    return 384 * (pair // 2) + LANES * (pair % 2)


def mask_heads(src_ref, dst_ref):
    heads, _, window = dst_ref.shape
    column = lax.broadcasted_iota(jnp.int32, (1, window), 1)
    for head in range(heads):
        low = window_start(head // 2)
        at = head * HD - low
        keep = jnp.where((column >= at) & (column < at + HD), 1.0, 0.0).astype(jnp.bfloat16)
        dst_ref[head] = src_ref[:, low : low + window] * keep


def frame_tiles(bounds_ref, bias_ref, offset, tile, body):
    frames, tokens = bias_ref.shape
    begin = bounds_ref[0:1, :] + offset
    end = bounds_ref[1:2, :] + offset
    for index in range(frames // tile):
        low = index * tile
        touch = (begin < low + tile) & (end > low)
        active = jnp.max(jnp.where(touch, 1.0, 0.0)) > 0.0

        @pl.when(active)
        def _():
            row = low + lax.broadcasted_iota(jnp.int32, (tile, tokens), 0)
            inside = (row >= begin) & (row < end)
            bias_ref[low : low + tile, :] = jnp.where(inside, 0.0, masked_fill)
            body(low)


def stats_kernel(offsets, tile, scale, k_ref, v_ref, *refs):
    guests = len(offsets)
    inputs, outputs = refs[: 3 * guests], refs[3 * guests : 4 * guests]
    qm_ref, um_ref, bias_ref = refs[4 * guests :]
    heads, tokens, window = qm_ref.shape
    for guest, offset in enumerate(offsets):
        q_ref, u_ref, b_ref = inputs[3 * guest : 3 * guest + 3]
        out = outputs[guest]
        mask_heads(q_ref, qm_ref)
        mask_heads(u_ref, um_ref)
        out[0:heads, :] = jnp.full((heads, tokens), masked_fill, jnp.float32)
        out[heads:, :] = jnp.zeros((2 * heads, tokens), jnp.float32)

        def body(low):
            def pair_step(pair, carry):
                cols = pl.ds(pl.multiple_of(window_start(pair), LANES), window)
                keys = k_ref[low : low + tile, cols]
                values = v_ref[low : low + tile, cols]
                bias = bias_ref[low : low + tile, :]
                for side in range(2):
                    head = 2 * pair + side
                    scores = contract_last(keys, qm_ref[head]) + bias
                    slopes = contract_last(values, um_ref[head])
                    old = out[pl.ds(head, 1), :]
                    new = jnp.maximum(old, jnp.max(scores, 0, keepdims=True))
                    fade = jnp.exp((old - new) * scale)
                    expos = jnp.exp((scores - new) * scale)
                    out[pl.ds(head, 1), :] = new
                    out[pl.ds(heads + head, 1), :] = out[
                        pl.ds(heads + head, 1), :
                    ] * fade + jnp.sum(expos, 0, keepdims=True)
                    out[pl.ds(2 * heads + head, 1), :] = out[
                        pl.ds(2 * heads + head, 1), :
                    ] * fade + jnp.sum(expos * slopes, 0, keepdims=True)
                return carry

            lax.fori_loop(0, heads // 2, pair_step, 0)

        frame_tiles(b_ref, bias_ref, offset, tile, body)


def grads_kernel(offsets, tile, scale, n_stats, final, k_ref, v_ref, kt_ref, *refs):
    guests = len(offsets)
    per = 3 + n_stats
    inputs, refs = refs[: per * guests], refs[per * guests :]
    if final:
        dk_in, dv_in, dk_out, dv_out, dq_out = refs[:5]
        dq_outs = [dq_out]
        qm_ref, um_ref, bias_ref, norm_ref, dqt_ref, dk_ref, dv_ref = refs[5:]
        dk_ref[...] = dk_in[...]
        dv_ref[...] = dv_in[...]
    else:
        dk_ref, dv_ref = refs[:2]
        dq_outs = refs[2 : 2 + guests]
        qm_ref, um_ref, bias_ref, norm_ref, dqt_ref = refs[2 + guests :]
        dk_ref[...] = jnp.zeros_like(dk_ref)
        dv_ref[...] = jnp.zeros_like(dv_ref)
    heads, tokens, window = qm_ref.shape
    for guest, offset in enumerate(offsets):
        q_ref, u_ref, b_ref = inputs[per * guest : per * guest + 3]
        stats = [r[...] for r in inputs[per * guest + 3 : per * guest + per]]
        peak = stats[0][0:heads]
        for one in stats[1:]:
            peak = jnp.maximum(peak, one[0:heads])
        total = jnp.zeros_like(peak)
        weighted = jnp.zeros_like(peak)
        for one in stats:
            factor = jnp.exp((one[0:heads] - peak) * scale)
            total = total + one[heads : 2 * heads] * factor
            weighted = weighted + one[2 * heads :] * factor
        total = jnp.where(total > 0.0, total, 1.0)
        norm_ref[0:heads, :] = peak * scale + jnp.log(total)
        norm_ref[heads:, :] = weighted / total
        mask_heads(q_ref, qm_ref)
        mask_heads(u_ref, um_ref)
        dqt_ref[...] = jnp.zeros_like(dqt_ref)

        def body(low):
            def pair_step(pair, carry):
                cols = pl.ds(pl.multiple_of(window_start(pair), LANES), window)
                keys = k_ref[low : low + tile, cols]
                values = v_ref[low : low + tile, cols]
                inside = bias_ref[low : low + tile, :] == 0.0
                key_term = value_term = None
                for side in range(2):
                    head = 2 * pair + side
                    scores = contract_last(keys, qm_ref[head])
                    slopes = contract_last(values, um_ref[head])
                    log_total = norm_ref[pl.ds(head, 1), :]
                    delta = norm_ref[pl.ds(heads + head, 1), :]
                    probs = jnp.where(inside, jnp.exp(scores * scale - log_total), 0.0)
                    grad = (probs * ((slopes - delta) * scale)).astype(jnp.bfloat16)
                    key_one = mm(grad, qm_ref[head])
                    value_one = mm(probs.astype(jnp.bfloat16), um_ref[head])
                    key_term = key_one if side == 0 else key_term + key_one
                    value_term = value_one if side == 0 else value_term + value_one
                    rows = pl.ds(pl.multiple_of(head * HD, HD // 3), HD)
                    dqt_ref[rows, :] += mm(kt_ref[rows, low : low + tile], grad)
                dk_ref[low : low + tile, cols] += key_term
                dv_ref[low : low + tile, cols] += value_term
                return carry

            lax.fori_loop(0, heads // 2, pair_step, 0)

        frame_tiles(b_ref, bias_ref, offset, tile, body)
        dq_outs[guest][...] = dqt_ref[...].T.astype(dq_outs[guest].dtype)
    if final:
        dk_out[...] = dk_ref[...].astype(jnp.bfloat16)
        dv_out[...] = dv_ref[...].astype(jnp.bfloat16)


def conv_kernel(block, h_ref, before_ref, after_ref, taps_ref, out_ref, x_ref, w_ref):
    chunks, rows, _ = x_ref.shape
    frames = rows - 2 * HALO
    for chunk in range(chunks):
        cols = slice(chunk * LANES, (chunk + 1) * LANES)
        x_ref[chunk, 0:HALO, :] = before_ref[:, cols].astype(jnp.float32)
        x_ref[chunk, HALO : HALO + frames, :] = h_ref[:, cols].astype(jnp.float32)
        x_ref[chunk, HALO + frames :, :] = after_ref[:, cols].astype(jnp.float32)
        w_ref[chunk, 0:KERNEL, :] = taps_ref[:, cols].astype(jnp.float32)
    for chunk in range(chunks):
        cols = slice(chunk * LANES, (chunk + 1) * LANES)

        def step(index, carry):
            low = pl.multiple_of(index * block, block)
            acc = x_ref[chunk, pl.ds(low + HALO, block), :]
            for tap in range(KERNEL):
                acc = acc + w_ref[chunk, tap : tap + 1, :] * x_ref[
                    chunk, pl.ds(low + HALO + HALF - tap, block), :
                ]
            out_ref[pl.ds(low, block), cols] = acc.astype(jnp.bfloat16)
            return carry

        lax.fori_loop(0, frames // block, step, 0)


def tile_of(frames):
    for tile in (256, 128, 64, 32, 16):
        if frames % tile == 0:
            return tile
    return frames


def params(mib=None):
    return pltpu.CompilerParams(vmem_limit_bytes=None if mib is None else mib << 20)


def attention(queries, upstream, bounds, frame_keys, frame_values):
    frames, width = frame_keys.shape
    tokens = queries.shape[0]
    heads = width // HD
    window = window_of(width)
    scale = 1.0 / math.sqrt(HD)
    tile = tile_of(frames)
    base = lax.axis_index("tm") * frames
    local = (bounds - base).T
    f32, bf16 = jnp.float32, jnp.bfloat16
    own = (queries, upstream, local)
    prev = tuple(shifted(x, "tm", 1) for x in own)
    after = tuple(shifted(x, "tm", -1) for x in own)
    keys_t = frame_keys.T
    shape = jax.ShapeDtypeStruct
    masks = [
        pltpu.VMEM((heads, tokens, window), bf16),
        pltpu.VMEM((heads, tokens, window), bf16),
        pltpu.VMEM((frames, tokens), f32),
    ]
    stat = shape((3 * heads, tokens), f32)
    work = 2 * tokens * frames * width

    def stats(offsets, guests):
        out = pl.pallas_call(
            functools.partial(stats_kernel, offsets, tile, scale),
            out_shape=[stat] * len(offsets),
            in_specs=[VMEM] * (2 + 3 * len(offsets)),
            out_specs=[VMEM] * len(offsets),
            scratch_shapes=masks,
            compiler_params=params(24),
            cost_estimate=pl.CostEstimate(
                flops=5 * work * len(offsets), bytes_accessed=4 * frames * width, transcendentals=0
            ),
            name="stats%d" % len(offsets),
        )(frame_keys, frame_values, *[x for guest in guests for x in guest])
        return list(out)

    (own_stats,) = stats((0,), (own,))
    prev_own = shifted(own_stats, "tm", 1)
    after_own = shifted(own_stats, "tm", -1)
    prev_stats, after_stats = stats((-frames, frames), (prev, after))
    from_after = shifted(prev_stats, "tm", -1)
    from_prev = shifted(after_stats, "tm", 1)
    position = lax.axis_index("tm")
    last = lax.axis_size("tm") - 1
    empty = jnp.where(jnp.arange(3 * heads) < heads, masked_fill, 0.0).astype(f32)[:, None]
    from_prev = jnp.where(position == 0, empty, from_prev)
    from_after = jnp.where(position == last, empty, from_after)

    grad_scratch = [
        pltpu.VMEM((2 * heads, tokens), f32),
        pltpu.VMEM((width, tokens), f32),
    ]
    accs = [pltpu.VMEM((frames, width), f32)] * 2
    dk, dv, prev_dq, after_dq = pl.pallas_call(
        functools.partial(grads_kernel, (-frames, frames), tile, scale, 2, False),
        out_shape=[shape((frames, width), f32)] * 2 + [shape((tokens, width), bf16)] * 2,
        in_specs=[VMEM] * 13,
        out_specs=[VMEM] * 4,
        scratch_shapes=masks + grad_scratch,
        compiler_params=params(32),
        cost_estimate=pl.CostEstimate(
            flops=20 * work, bytes_accessed=20 * frames * width, transcendentals=0
        ),
        name="grads2",
    )(frame_keys, frame_values, keys_t, *prev, prev_stats, prev_own, *after, after_stats, after_own)
    back_prev = shifted(prev_dq, "tm", -1)
    back_after = shifted(after_dq, "tm", 1)
    key_low, value_low, own_dq = pl.pallas_call(
        functools.partial(grads_kernel, (0,), tile, scale, 3, True),
        out_shape=[shape((frames, width), bf16)] * 2 + [shape((tokens, width), f32)],
        in_specs=[VMEM] * 11,
        out_specs=[VMEM] * 3,
        scratch_shapes=masks + grad_scratch + accs,
        compiler_params=params(40),
        cost_estimate=pl.CostEstimate(
            flops=10 * work, bytes_accessed=20 * frames * width, transcendentals=0
        ),
        name="grads1",
    )(frame_keys, frame_values, keys_t, *own, own_stats, from_prev, from_after, dk, dv)
    query_gradient = own_dq + back_prev.astype(f32) + back_after.astype(f32)
    return key_low, value_low, query_gradient.astype(bf16)


def depthwise(hidden_gradient, kernel_taps):
    frames, width = hidden_gradient.shape
    before = shifted(hidden_gradient[frames - HALO :], "tm", 1)
    after = shifted(hidden_gradient[:HALO], "tm", -1)
    chunks = width // LANES
    return pl.pallas_call(
        functools.partial(conv_kernel, tile_of(frames) // 4),
        out_shape=jax.ShapeDtypeStruct((frames, width), jnp.bfloat16),
        in_specs=[VMEM] * 4,
        out_specs=VMEM,
        scratch_shapes=[
            pltpu.VMEM((chunks, frames + 2 * HALO, LANES), jnp.float32),
            pltpu.VMEM((chunks, KERNEL + 1, LANES), jnp.float32),
        ],
        compiler_params=params(16),
        name="conv",
    )(hidden_gradient, before, after, kernel_taps)


def plain_depthwise(hidden_gradient, kernel_taps):
    frames = hidden_gradient.shape[0]
    before = shifted(hidden_gradient[frames - HALF :], "tm", 1)
    after = shifted(hidden_gradient[:HALF], "tm", -1)
    padded = jnp.concatenate([before, hidden_gradient, after], 0).astype(jnp.float32)
    weights = kernel_taps.astype(jnp.float32)
    result = hidden_gradient.astype(jnp.float32)
    for tap in range(KERNEL):
        lower = 2 * HALF - tap
        result = result + weights[tap] * padded[lower : lower + frames]
    return result.astype(jnp.bfloat16)


def mp_sum(part):
    if lax.axis_size("mp") == 2:
        other = lax.ppermute(part, "mp", [(0, 1), (1, 0)])
        return part.astype(jnp.float32) + other.astype(jnp.float32)
    return lax.psum(part, "mp").astype(jnp.float32)


def mp_scatter(part, width):
    me = lax.axis_index("mp")
    if lax.axis_size("mp") == 2:
        mine = lax.dynamic_slice_in_dim(part, me * width, width, 1)
        theirs = lax.dynamic_slice_in_dim(part, (1 - me) * width, width, 1)
        other = lax.ppermute(theirs, "mp", [(0, 1), (1, 0)])
        return mine.astype(jnp.float32) + other.astype(jnp.float32)
    return lax.psum_scatter(part, "mp", scatter_dimension=1, tiled=True).astype(jnp.float32)


def feed_forward(key_low, value_low, hidden_pre, expand_weight, shrink_weight, key_weight, value_weight):
    frames, width = key_low.shape
    pieces = 2 if frames % 32 == 0 else 1
    size = frames // pieces
    me = lax.axis_index("mp")
    sums = []
    for piece in range(pieces):
        rows = slice(piece * size, (piece + 1) * size)
        part = contract_last(key_low[rows], key_weight) + contract_last(value_low[rows], value_weight)
        sums.append(mp_sum(part.astype(jnp.bfloat16)))
    out = []
    for piece in range(pieces):
        rows = slice(piece * size, (piece + 1) * size)
        act = 0.5 * contract_last(sums[piece].astype(jnp.bfloat16), shrink_weight)
        pre = (act * silu_slope(hidden_pre[rows].astype(jnp.float32))).astype(jnp.bfloat16)
        back = mp_scatter(contract_last(pre, expand_weight).astype(jnp.bfloat16), width)
        mine = lax.dynamic_slice_in_dim(sums[piece], me * width, width, 1)
        out.append((mine + back).astype(jnp.bfloat16))
    return jnp.concatenate(out, 0) if pieces > 1 else out[0]


def shards(
    queries,
    upstream,
    bounds,
    frame_keys,
    frame_values,
    hidden_pre,
    expand_weight,
    shrink_weight,
    key_weight,
    value_weight,
    kernel_taps,
):
    key_low, value_low, query_gradient = attention(
        queries, upstream, bounds, frame_keys, frame_values
    )
    hidden_gradient = feed_forward(
        key_low, value_low, hidden_pre, expand_weight, shrink_weight, key_weight, value_weight
    )
    if hidden_gradient.shape[1] % LANES == 0:
        frame_gradient = depthwise(hidden_gradient, kernel_taps)
    else:
        frame_gradient = plain_depthwise(hidden_gradient, kernel_taps)
    return (frame_gradient, query_gradient)


def solution(mesh):
    placed = (
        P("tm", "mp"),
        P("tm", "mp"),
        P("tm", None),
        P("tm", "mp"),
        P("tm", "mp"),
        P("tm", "mp"),
        P(None, "mp"),
        P("mp", None),
        P(None, "mp"),
        P(None, "mp"),
        P(None, "mp"),
    )
    return jax.shard_map(
        shards,
        mesh=mesh,
        in_specs=placed,
        out_specs=(P("tm", "mp"), P("tm", "mp")),
        check_vma=False,
    )
```

time: 383 us -> 178 us (0.46)
  the two profiles are of different devices: /device:TPU:8 before, /device:TPU:12 now
where the time goes in v1:
time: 178 us; the launch traced here: 177 us
  Pallas kernels  45.7 us (26%)
  starting transfers between devices  44.9 us (25%)
  waiting for transfers between devices  42.5 us (24%)
  matrix products  24.9 us (14%)
  local copies, waits for them, and re-layouts  10.9 us (6%)
  other arithmetic  7.28 us (4%)
    ppermute x14, starting transfers between devices, shifted(): return lax.ppermute(value, axis, pairs)  44.5 us
    ppermute x14, waiting for transfers between devices, shifted(): return lax.ppermute(value, axis, pairs)  42.5 us
    dot_general x6, matrix products, contract_last(): lax.dot_general(left, right, (((1,), (1,)), ((), ())), preferred_element_...  24.9 us
    pallas_call x2, Pallas kernels, stats(): pl.pallas_call(functools.partial(stats_kernel, offsets, tile, scale), out...  14.1 us
    pallas_call x1, Pallas kernels, attention(): pl.pallas_call(functools.partial(grads_kernel, (-frames, frames), tile, s...  12.6 us
    pallas_call x1, Pallas kernels, attention(): pl.pallas_call(functools.partial(grads_kernel, (0,), tile, scale, 3, True...  11 us
    unnamed x55, local copies, waits for them, and re-layouts  9.85 us
    pallas_call x1, Pallas kernels, depthwise(): pl.pallas_call(functools.partial(conv_kernel, tile_of(frames) // 4), out_...  8.01 us
  transfers between devices with their start and end apart: 18, of which 5 were waited for; matrix products, arithmetic and copies ran while one was open for 18% of the time, Pallas kernels for 15%

profile of v1, /device:TPU:12, one launch (start us, length us, event | category | flops | bytes accessed | tf_op | source)
XLA Modules:
  0.0 177.4 jit_solution(10410474895455299850)
XLA Ops:
  0.6 3.5 %collective-permute-start = (bf16[256,768]{1,0:T(8,128)(2,1)}, bf16[256,768]{1,0:T(8,128)(2,1)}, u32[]{:S(2)}, u32[]{:S(2)}) collective-permute-start(bf16[256,768]{1,0:T(8,128)(2,1)} %refs_0_.3), channel_id=1, source_target_pairs={{0,2},{2,4},{4,6},{6,8},{8,10},{10,12},{12,14},{14,16},{16,18},{18... | collective-permute-start | bytes 1179656 | tf_op jit(solution)/shard_map/ppermute | solution.py:23
  4.2 3.3 %collective-permute-start.3 = (bf16[256,768]{1,0:T(8,128)(2,1)}, bf16[256,768]{1,0:T(8,128)(2,1)}, u32[]{:S(2)}, u32[]{:S(2)}) collective-permute-start(bf16[256,768]{1,0:T(8,128)(2,1)} %refs_0_.3), channel_id=1, source_target_pairs={{2,0},{4,2},{6,4},{8,6},{10,8},{12,10},{14,12},{16,14},{18,16},{20... | collective-permute-start | bytes 1179656 | tf_op jit(solution)/shard_map/ppermute | solution.py:23
  7.5 2.5 %collective-permute-start.1 = (bf16[256,768]{1,0:T(8,128)(2,1)}, bf16[256,768]{1,0:T(8,128)(2,1)}, u32[]{:S(2)}, u32[]{:S(2)}) collective-permute-start(bf16[256,768]{1,0:T(8,128)(2,1)} %refs_1_.3), channel_id=1, source_target_pairs={{0,2},{2,4},{4,6},{6,8},{8,10},{10,12},{12,14},{14,16},{16,18},{18... | collective-permute-start | bytes 1179656 | tf_op jit(solution)/shard_map/ppermute | solution.py:23
  10.1 4.2 %collective-permute-start.4 = (bf16[256,768]{1,0:T(8,128)(2,1)}, bf16[256,768]{1,0:T(8,128)(2,1)}, u32[]{:S(2)}, u32[]{:S(2)}) collective-permute-start(bf16[256,768]{1,0:T(8,128)(2,1)} %refs_1_.3), channel_id=1, source_target_pairs={{2,0},{4,2},{6,4},{8,6},{10,8},{12,10},{14,12},{16,14},{18,16},{20... | collective-permute-start | bytes 1179656 | tf_op jit(solution)/shard_map/ppermute | solution.py:23
  15.0 2.9 %collective-permute-start.2 = (s32[2,256]{1,0:T(2,128)S(1)}, s32[2,256]{1,0:T(2,128)S(1)}, u32[]{:S(2)}, u32[]{:S(2)}) collective-permute-start(s32[2,256]{1,0:T(2,128)S(1)} %subtract_bitcast_fusion.refs_2_), channel_id=1, source_target_pairs={{0,2},{2,4},{4,6},{6,8},{8,10},{10,12},{12,14},{14,16},{16,18},{18... | collective-permute-start | bytes 6152 | tf_op jit(solution)/shard_map/ppermute | solution.py:23
  22.4 6.1 %stats1.1.refs_3_ = f32[24,256]{1,0:T(8,128)S(1)} custom-call(bf16[768,768]{1,0:T(8,128)(2,1)S(1)} %copy-done.1, bf16[768,768]{1,0:T(8,128)(2,1)S(1)} %copy-done.7, bf16[256,768]{1,0:T(8,128)(2,1)S(1)} %copy-done.10, bf16[256,768]{1,0:T(8,128)(2,1)S(1)} %copy-done.12, s32[2,256]{1,0:T(2,128)S(1)} %subtract_bitcast_fusion.refs_2_), custom_call_target="tpu_custom_call" | custom-call | flops 1509949440 | bytes 2359296 | tf_op jit(solution)/shard_map/stats1/pallas_call | solution.py:247
  29.1 10.8 %collective-permute-done.2.refs_2_ = s32[2,256]{1,0:T(2,128)S(1)} collective-permute-done((s32[2,256]{1,0:T(2,128)S(1)}, s32[2,256]{1,0:T(2,128)S(1)}, u32[]{:S(2)}, u32[]{:S(2)}) %collective-permute-start.2) | collective-permute-done | bytes 2080 | tf_op jit(solution)/shard_map/ppermute | solution.py:23
  40.0 2.5 %collective-permute-start.5 = (s32[2,256]{1,0:T(2,128)S(1)}, s32[2,256]{1,0:T(2,128)S(1)}, u32[]{:S(2)}, u32[]{:S(2)}) collective-permute-start(s32[2,256]{1,0:T(2,128)S(1)} %subtract_bitcast_fusion.refs_2_), channel_id=1, source_target_pairs={{2,0},{4,2},{6,4},{8,6},{10,8},{12,10},{14,12},{16,14},{18,16},{20... | collective-permute-start | bytes 6152 | tf_op jit(solution)/shard_map/ppermute | solution.py:23
  42.5 1.5 copy.13
  44.0 1.5 collective-permute-done.5.refs_5_.refs_7_
  45.4 4.3 %collective-permute-start.8 = (f32[24,256]{1,0:T(8,128)}, f32[24,256]{1,0:T(8,128)S(1)}, u32[]{:S(2)}, u32[]{:S(2)}) collective-permute-start(f32[24,256]{1,0:T(8,128)} %copy-done.18), channel_id=1, source_target_pairs={{0,2},{2,4},{4,6},{6,8},{8,10},{10,12},{12,14},{14,16},{16,18},{18... | collective-permute-start | bytes 73736 | tf_op jit(solution)/shard_map/ppermute | solution.py:23
  49.7 2.4 %collective-permute-start.9 = (f32[24,256]{1,0:T(8,128)}, f32[24,256]{1,0:T(8,128)S(1)}, u32[]{:S(2)}, u32[]{:S(2)}) collective-permute-start(f32[24,256]{1,0:T(8,128)} %copy-done.18), channel_id=1, source_target_pairs={{2,0},{4,2},{6,4},{8,6},{10,8},{12,10},{14,12},{16,14},{18,16},{20... | collective-permute-start | bytes 73736 | tf_op jit(solution)/shard_map/ppermute | solution.py:23
  53.5 8.0 %stats2.1 = (f32[24,256]{1,0:T(8,128)S(1)}, f32[24,256]{1,0:T(8,128)S(1)}) custom-call(bf16[768,768]{1,0:T(8,128)(2,1)S(1)} %copy-done.2, bf16[768,768]{1,0:T(8,128)(2,1)S(1)} %copy-done.8, bf16[256,768]{1,0:T(8,128)(2,1)} %collective-permute-done.refs_0_, bf16[256,768]{1,0:T(8,128)(2,1)} %collective-permute-done.1.refs_1_, ...), custom_call_target="tpu_custom_call" | custom-call | flops 3019898880 | bytes 2359296 | tf_op jit(solution)/shard_map/stats2/pallas_call | solution.py:247
  61.5 1.9 %collective-permute-start.6 = (f32[24,256]{1,0:T(8,128)S(1)}, f32[24,256]{1,0:T(8,128)S(1)}, u32[]{:S(2)}, u32[]{:S(2)}) collective-permute-start(f32[24,256]{1,0:T(8,128)S(1)} %get-tuple-element.11.refs_8_), channel_id=1, source_target_pairs={{0,2},{2,4},{4,6},{6,8},{8,10},{10,12},{12,14},{14,16},{16,18},{18... | collective-permute-start | bytes 73736 | tf_op jit(solution)/shard_map/ppermute | solution.py:23
  63.5 4.8 %collective-permute-start.7 = (f32[24,256]{1,0:T(8,128)S(1)}, f32[24,256]{1,0:T(8,128)S(1)}, u32[]{:S(2)}, u32[]{:S(2)}) collective-permute-start(f32[24,256]{1,0:T(8,128)S(1)} %get-tuple-element.12.refs_3_), channel_id=1, source_target_pairs={{2,0},{4,2},{6,4},{8,6},{10,8},{12,10},{14,12},{16,14},{18,16},{20... | collective-permute-start | bytes 73736 | tf_op jit(solution)/shard_map/ppermute | solution.py:23
  68.4 12.6 %grads2.1 = (f32[768,768]{1,0:T(8,128)S(1)}, f32[768,768]{1,0:T(8,128)S(1)}, bf16[256,768]{1,0:T(8,128)(2,1)S(1)}, bf16[256,768]{1,0:T(8,128)(2,1)S(1)}) custom-call(bf16[768,768]{1,0:T(8,128)(2,1)S(1)} %copy-done.2, bf16[768,768]{1,0:T(8,128)(2,1)S(1)} %copy-done.9, bf16[768,768]{1,0:T(8,128)(2,1)S(1)} %bitcast.11, ...), custom_call_target="tpu_custom_call" | custom-call | flops 6039797760 | bytes 11796480 | tf_op jit(solution)/shard_map/grads2/pallas_call | solution.py:278
  81.1 11.0 %grads1.1 = (bf16[768,768]{1,0:T(8,128)(2,1)S(1)}, bf16[768,768]{1,0:T(8,128)(2,1)S(1)}, f32[256,768]{1,0:T(8,128)S(1)}) custom-call(bf16[768,768]{1,0:T(8,128)(2,1)S(1)} %copy-done.2, bf16[768,768]{1,0:T(8,128)(2,1)S(1)} %copy-done.9, bf16[768,768]{1,0:T(8,128)(2,1)S(1)} %bitcast.12, bf16[256,768]{1,0:T(8,128)(2,1)S(1)} %copy-done.11, ...), custom_call_target="tpu_custom_call" | custom-call | flops 3019898880 | bytes 11796480 | tf_op jit(solution)/shard_map/grads1/pallas_call | solution.py:292
  94.9 2.2 %fusion.4 = bf16[384,1536]{1,0:T(8,128)(2,1)} fusion(f32[384,1536]{1,0:T(8,128)S(1)} %fusion.25, bf16[1536,768]{1,0:T(8,128)(2,1)S(1)} %copy-done.25, bf16[768,768]{1,0:T(8,128)(2,1)S(1)} %get-tuple-element.15), kind=kOutput, calls=%fused_computation.14 | convolution fusion | flops 907149312 | bytes 6488064 | tf_op jit(solution)/shard_map/dot_general | solution.py:27
  97.1 3.8 %collective-permute-start.16 = (bf16[256,768]{1,0:T(8,128)(2,1)S(1)}, bf16[256,768]{1,0:T(8,128)(2,1)S(1)}, u32[]{:S(2)}, u32[]{:S(2)}) collective-permute-start(bf16[256,768]{1,0:T(8,128)(2,1)S(1)} %copy-done.17), channel_id=1, source_target_pairs={{2,0},{4,2},{6,4},{8,6},{10,8},{12,10},{14,12},{16,14},{18,16},{20... | collective-permute-start | bytes 1179656 | tf_op jit(solution)/shard_map/ppermute | solution.py:23
  100.9 2.3 %collective-permute-start.17 = (bf16[256,768]{1,0:T(8,128)(2,1)S(1)}, bf16[256,768]{1,0:T(8,128)(2,1)S(1)}, u32[]{:S(2)}, u32[]{:S(2)}) collective-permute-start(bf16[256,768]{1,0:T(8,128)(2,1)S(1)} %copy-done.15), channel_id=1, source_target_pairs={{0,2},{2,4},{4,6},{6,8},{8,10},{10,12},{12,14},{14,16},{16,18},{18... | collective-permute-start | bytes 1179656 | tf_op jit(solution)/shard_map/ppermute | solution.py:23
  103.2 2.2 %fusion.22 = f32[384,1536]{1,0:T(8,128)S(1)} fusion(bf16[1536,768]{1,0:T(8,128)(2,1)S(1)} %copy-done, bf16[768,768]{1,0:T(8,128)(2,1)} %copy-done.22), kind=kOutput, calls=%fused_computation.34 | convolution fusion | flops 905969664 | bytes 5308416 | tf_op jit(solution)/shard_map/dot_general | solution.py:27
  105.4 2.1 %fusion.5 = bf16[384,1536]{1,0:T(8,128)(2,1)} fusion(f32[384,1536]{1,0:T(8,128)S(1)} %fusion.22, bf16[1536,768]{1,0:T(8,128)(2,1)S(1)} %copy-done.26, bf16[768,768]{1,0:T(8,128)(2,1)S(1)} %copy-done.21), kind=kOutput, calls=%fused_computation.15 | convolution fusion | flops 907149312 | bytes 6488064 | tf_op jit(solution)/shard_map/dot_general | solution.py:27
  107.6 2.8 %collective-permute-done.16 = bf16[256,768]{1,0:T(8,128)(2,1)S(1)} collective-permute-done((bf16[256,768]{1,0:T(8,128)(2,1)S(1)}, bf16[256,768]{1,0:T(8,128)(2,1)S(1)}, u32[]{:S(2)}, u32[]{:S(2)}) %collective-permute-start.16) | collective-permute-done | bytes 393248 | tf_op jit(solution)/shard_map/ppermute | solution.py:23
  110.5 24.7 %collective-permute-done.17 = bf16[256,768]{1,0:T(8,128)(2,1)S(1)} collective-permute-done((bf16[256,768]{1,0:T(8,128)(2,1)S(1)}, bf16[256,768]{1,0:T(8,128)(2,1)S(1)}, u32[]{:S(2)}, u32[]{:S(2)}) %collective-permute-start.17) | collective-permute-done | bytes 393248 | tf_op jit(solution)/shard_map/ppermute | solution.py:23
  136.1 8.7 %convolution_convert_fusion.1 = bf16[384,1536]{1,0:T(8,128)(2,1)S(1)} fusion(bf16[1536,1536]{1,0:T(8,128)(2,1)} %param.17, bf16[1536,1536]{1,0:T(8,128)(2,1)} %param.18, bf16[768,1536]{1,0:T(8,128)(2,1)} %param.16, bf16[384,1536]{1,0:T(8,128)(2,1)} %collective-permute-done.10, bf16[384,1536]{1,0:T(8,128)(2,1)} %fusion.4), kind=kOutput, calls=%fused_computation.11 | convolution fusion | flops 3633315840 | bytes 14155776 | tf_op jit(solution)/shard_map/dot_general | solution.py:27
  146.0 8.7 %convolution_convert_fusion = bf16[384,1536]{1,0:T(8,128)(2,1)S(1)} fusion(bf16[1536,1536]{1,0:T(8,128)(2,1)} %param.17, bf16[1536,1536]{1,0:T(8,128)(2,1)} %param.18, bf16[768,1536]{1,0:T(8,128)(2,1)} %param.16, bf16[384,1536]{1,0:T(8,128)(2,1)} %collective-permute-done.12, bf16[384,1536]{1,0:T(8,128)(2,1)} %fusion.5), kind=kOutput, calls=%fused_computation.10 | convolution fusion | flops 3633315840 | bytes 14155776 | tf_op jit(solution)/shard_map/dot_general | solution.py:27
  155.0 2.0 %convert_add_fusion.1 = f32[384,1536]{1,0:T(8,128)S(1)} fusion(bf16[384,1536]{1,0:T(8,128)(2,1)} %collective-permute-done.10, bf16[384,1536]{1,0:T(8,128)(2,1)} %fusion.4), kind=kLoop, calls=%fused_computation.27 | loop fusion | flops 1769472 | bytes 4718592 | tf_op jit(solution)/shard_map/add | solution.py:343
  157.0 2.1 %convert_add_fusion = f32[384,1536]{1,0:T(8,128)S(1)} fusion(bf16[384,1536]{1,0:T(8,128)(2,1)} %collective-permute-done.12, bf16[384,1536]{1,0:T(8,128)(2,1)} %fusion.5), kind=kLoop, calls=%fused_computation.26 | loop fusion | flops 1769472 | bytes 4718592 | tf_op jit(solution)/shard_map/add | solution.py:343
  160.4 2.1 %collective-permute-start.15 = (bf16[16,768]{1,0:T(8,128)(2,1)S(1)}, bf16[16,768]{1,0:T(8,128)(2,1)S(1)}, u32[]{:S(2)}, u32[]{:S(2)}) collective-permute-start(bf16[16,768]{1,0:T(8,128)(2,1)S(1)} %slice.33), channel_id=1, source_target_pairs={{2,0},{4,2},{6,4},{8,6},{10,8},{12,10},{14,12},{16,14},{18,16},{20... | collective-permute-start | bytes 73736 | tf_op jit(solution)/shard_map/ppermute | solution.py:23
  162.8 3.9 %collective-permute-start.14 = (bf16[16,768]{1,0:T(8,128)(2,1)S(1)}, bf16[16,768]{1,0:T(8,128)(2,1)S(1)}, u32[]{:S(2)}, u32[]{:S(2)}) collective-permute-start(bf16[16,768]{1,0:T(8,128)(2,1)S(1)} %slice.32), channel_id=1, source_target_pairs={{0,2},{2,4},{4,6},{6,8},{8,10},{10,12},{12,14},{14,16},{16,18},{18... | collective-permute-start | bytes 73736 | tf_op jit(solution)/shard_map/ppermute | solution.py:23
  166.8 2.6 %collective-permute-done.14.before_ref = bf16[16,768]{1,0:T(8,128)(2,1)S(1)} collective-permute-done((bf16[16,768]{1,0:T(8,128)(2,1)S(1)}, bf16[16,768]{1,0:T(8,128)(2,1)S(1)}, u32[]{:S(2)}, u32[]{:S(2)}) %collective-permute-start.14) | collective-permute-done | bytes 24608 | tf_op jit(solution)/shard_map/ppermute | solution.py:23
  169.4 8.0 %conv.1 = bf16[768,768]{1,0:T(8,128)(2,1)} custom-call(bf16[768,768]{1,0:T(8,128)(2,1)S(1)} %pad_maximum_fusion.h_ref, bf16[16,768]{1,0:T(8,128)(2,1)S(1)} %collective-permute-done.14.before_ref, bf16[16,768]{1,0:T(8,128)(2,1)S(1)} %collective-permute-done.15.after_ref, bf16[31,768]{1,0:T(8,128)(2,1)S(1)} %copy-done.6), custom_call_target="tpu_custom_call" | custom-call | tf_op jit(solution)/shard_map/conv/pallas_call | solution.py:313
  (83 shorter events, 14.2 us)
Async XLA Ops:
  0.6 91.5 %copy-start = (bf16[1536,768]{1,0:T(8,128)(2,1)S(1)}, bf16[1536,768]{1,0:T(8,128)(2,1)}, u32[]{:S(2)}) copy-start(bf16[1536,768]{1,0:T(8,128)(2,1)} %param.20) | copy-start | bytes 7077892
  0.6 49.1 %collective-permute-start = (bf16[256,768]{1,0:T(8,128)(2,1)}, bf16[256,768]{1,0:T(8,128)(2,1)}, u32[]{:S(2)}, u32[]{:S(2)}) collective-permute-start(bf16[256,768]{1,0:T(8,128)(2,1)} %refs_0_.3), channel_id=1, source_target_pairs={{0,2},{2,4},{4,6},{6,8},{8,10},{10,12},{12,14},{14,16},{16,18},{18... | collective-permute-start | bytes 1179656 | tf_op jit(solution)/shard_map/ppermute | solution.py:23
  4.2 48.0 %collective-permute-start.3 = (bf16[256,768]{1,0:T(8,128)(2,1)}, bf16[256,768]{1,0:T(8,128)(2,1)}, u32[]{:S(2)}, u32[]{:S(2)}) collective-permute-start(bf16[256,768]{1,0:T(8,128)(2,1)} %refs_0_.3), channel_id=1, source_target_pairs={{2,0},{4,2},{6,4},{8,6},{10,8},{12,10},{14,12},{16,14},{18,16},{20... | collective-permute-start | bytes 1179656 | tf_op jit(solution)/shard_map/ppermute | solution.py:23
  7.5 44.6 %collective-permute-start.1 = (bf16[256,768]{1,0:T(8,128)(2,1)}, bf16[256,768]{1,0:T(8,128)(2,1)}, u32[]{:S(2)}, u32[]{:S(2)}) collective-permute-start(bf16[256,768]{1,0:T(8,128)(2,1)} %refs_1_.3), channel_id=1, source_target_pairs={{0,2},{2,4},{4,6},{6,8},{8,10},{10,12},{12,14},{14,16},{16,18},{18... | collective-permute-start | bytes 1179656 | tf_op jit(solution)/shard_map/ppermute | solution.py:23
  10.1 42.2 %collective-permute-start.4 = (bf16[256,768]{1,0:T(8,128)(2,1)}, bf16[256,768]{1,0:T(8,128)(2,1)}, u32[]{:S(2)}, u32[]{:S(2)}) collective-permute-start(bf16[256,768]{1,0:T(8,128)(2,1)} %refs_1_.3), channel_id=1, source_target_pairs={{2,0},{4,2},{6,4},{8,6},{10,8},{12,10},{14,12},{16,14},{18,16},{20... | collective-permute-start | bytes 1179656 | tf_op jit(solution)/shard_map/ppermute | solution.py:23
  15.0 25.0 %collective-permute-start.2 = (s32[2,256]{1,0:T(2,128)S(1)}, s32[2,256]{1,0:T(2,128)S(1)}, u32[]{:S(2)}, u32[]{:S(2)}) collective-permute-start(s32[2,256]{1,0:T(2,128)S(1)} %subtract_bitcast_fusion.refs_2_), channel_id=1, source_target_pairs={{0,2},{2,4},{4,6},{6,8},{8,10},{10,12},{12,14},{14,16},{16,18},{18... | collective-permute-start | bytes 6152 | tf_op jit(solution)/shard_map/ppermute | solution.py:23
  22.4 20.1 %copy-start.2 = (bf16[768,768]{1,0:T(8,128)(2,1)S(1)}, bf16[768,768]{1,0:T(8,128)(2,1)}, u32[]{:S(2)}) copy-start(bf16[768,768]{1,0:T(8,128)(2,1)} %k_ref.7) | copy-start | bytes 3538948
  40.0 5.5 %collective-permute-start.5 = (s32[2,256]{1,0:T(2,128)S(1)}, s32[2,256]{1,0:T(2,128)S(1)}, u32[]{:S(2)}, u32[]{:S(2)}) collective-permute-start(s32[2,256]{1,0:T(2,128)S(1)} %subtract_bitcast_fusion.refs_2_), channel_id=1, source_target_pairs={{2,0},{4,2},{6,4},{8,6},{10,8},{12,10},{14,12},{16,14},{18,16},{20... | collective-permute-start | bytes 6152 | tf_op jit(solution)/shard_map/ppermute | solution.py:23
  44.0 24.4 %copy-start.3 = (bf16[768,768]{0,1:T(8,128)(2,1)S(1)}, bf16[768,768]{0,1:T(8,128)(2,1)}, u32[]{:S(2)}) copy-start(bf16[768,768]{0,1:T(8,128)(2,1)} %copy.13) | copy-start | bytes 3538948
  45.4 22.9 %collective-permute-start.8 = (f32[24,256]{1,0:T(8,128)}, f32[24,256]{1,0:T(8,128)S(1)}, u32[]{:S(2)}, u32[]{:S(2)}) collective-permute-start(f32[24,256]{1,0:T(8,128)} %copy-done.18), channel_id=1, source_target_pairs={{0,2},{2,4},{4,6},{6,8},{8,10},{10,12},{12,14},{14,16},{16,18},{18... | collective-permute-start | bytes 73736 | tf_op jit(solution)/shard_map/ppermute | solution.py:23
  49.7 18.6 %collective-permute-start.9 = (f32[24,256]{1,0:T(8,128)}, f32[24,256]{1,0:T(8,128)S(1)}, u32[]{:S(2)}, u32[]{:S(2)}) collective-permute-start(f32[24,256]{1,0:T(8,128)} %copy-done.18), channel_id=1, source_target_pairs={{2,0},{4,2},{6,4},{8,6},{10,8},{12,10},{14,12},{16,14},{18,16},{20... | collective-permute-start | bytes 73736 | tf_op jit(solution)/shard_map/ppermute | solution.py:23
  53.5 14.8 %copy-start.9 = (bf16[768,768]{1,0:T(8,128)(2,1)S(1)}, bf16[768,768]{1,0:T(8,128)(2,1)}, u32[]{:S(2)}) copy-start(bf16[768,768]{1,0:T(8,128)(2,1)} %v_ref.7) | copy-start | bytes 3538948
  61.5 19.4 %collective-permute-start.6 = (f32[24,256]{1,0:T(8,128)S(1)}, f32[24,256]{1,0:T(8,128)S(1)}, u32[]{:S(2)}, u32[]{:S(2)}) collective-permute-start(f32[24,256]{1,0:T(8,128)S(1)} %get-tuple-element.11.refs_8_), channel_id=1, source_target_pairs={{0,2},{2,4},{4,6},{6,8},{8,10},{10,12},{12,14},{14,16},{16,18},{18... | collective-permute-start | bytes 73736 | tf_op jit(solution)/shard_map/ppermute | solution.py:23
  63.5 17.5 %collective-permute-start.7 = (f32[24,256]{1,0:T(8,128)S(1)}, f32[24,256]{1,0:T(8,128)S(1)}, u32[]{:S(2)}, u32[]{:S(2)}) collective-permute-start(f32[24,256]{1,0:T(8,128)S(1)} %get-tuple-element.12.refs_3_), channel_id=1, source_target_pairs={{2,0},{4,2},{6,4},{8,6},{10,8},{12,10},{14,12},{16,14},{18,16},{20... | collective-permute-start | bytes 73736 | tf_op jit(solution)/shard_map/ppermute | solution.py:23
  68.3 12.7 %copy-start.11 = (bf16[256,768]{1,0:T(8,128)(2,1)S(1)}, bf16[256,768]{1,0:T(8,128)(2,1)}, u32[]{:S(2)}) copy-start(bf16[256,768]{1,0:T(8,128)(2,1)} %refs_0_.3) | copy-start | bytes 1179652
  68.4 12.7 %copy-start.13 = (bf16[256,768]{1,0:T(8,128)(2,1)S(1)}, bf16[256,768]{1,0:T(8,128)(2,1)}, u32[]{:S(2)}) copy-start(bf16[256,768]{1,0:T(8,128)(2,1)} %refs_1_.3) | copy-start | bytes 1179652
  68.4 12.7 %copy-start.19 = (f32[24,256]{1,0:T(8,128)S(1)}, f32[24,256]{1,0:T(8,128)}, u32[]{:S(2)}) copy-start(f32[24,256]{1,0:T(8,128)} %copy-done.18) | copy-start | bytes 73732
  80.9 11.1 %copy-start.14 = (bf16[256,768]{1,0:T(8,128)(2,1)}, bf16[256,768]{1,0:T(8,128)(2,1)S(1)}, u32[]{:S(2)}) copy-start(bf16[256,768]{1,0:T(8,128)(2,1)S(1)} %get-tuple-element.19) | copy-start | bytes 1179652
  80.9 11.1 %copy-start.16 = (bf16[256,768]{1,0:T(8,128)(2,1)}, bf16[256,768]{1,0:T(8,128)(2,1)S(1)}, u32[]{:S(2)}) copy-start(bf16[256,768]{1,0:T(8,128)(2,1)S(1)} %get-tuple-element.18) | copy-start | bytes 1179652
  94.9 5.9 %copy-start.15 = (bf16[256,768]{1,0:T(8,128)(2,1)S(1)}, bf16[256,768]{1,0:T(8,128)(2,1)}, u32[]{:S(2)}) copy-start(bf16[256,768]{1,0:T(8,128)(2,1)} %copy-done.14) | copy-start | bytes 1179652
  97.0 39.0 %collective-permute-start.10 = (bf16[384,1536]{1,0:T(8,128)(2,1)}, bf16[384,1536]{1,0:T(8,128)(2,1)}, u32[]{:S(2)}, u32[]{:S(2)}) collective-permute-start(bf16[384,1536]{1,0:T(8,128)(2,1)} %fusion.4), channel_id=1, source_target_pairs={{0,1},{1,0},{2,3},{3,2},{4,5},{5,4},{6,7},{7,6},{8,9},{9,8},{10,11... | collective-permute-start | bytes 3538952 | tf_op jit(solution)/shard_map/ppermute | solution.py:342
  97.1 13.4 %collective-permute-start.16 = (bf16[256,768]{1,0:T(8,128)(2,1)S(1)}, bf16[256,768]{1,0:T(8,128)(2,1)S(1)}, u32[]{:S(2)}, u32[]{:S(2)}) collective-permute-start(bf16[256,768]{1,0:T(8,128)(2,1)S(1)} %copy-done.17), channel_id=1, source_target_pairs={{2,0},{4,2},{6,4},{8,6},{10,8},{12,10},{14,12},{16,14},{18,16},{20... | collective-permute-start | bytes 1179656 | tf_op jit(solution)/shard_map/ppermute | solution.py:23
  100.8 4.5 %copy-start.21 = (bf16[768,768]{1,0:T(8,128)(2,1)S(1)}, bf16[768,768]{1,0:T(8,128)(2,1)}, u32[]{:S(2)}) copy-start(bf16[768,768]{1,0:T(8,128)(2,1)} %copy-done.20) | copy-start | bytes 3538948
  100.8 4.5 %copy-start.26 = (bf16[1536,768]{1,0:T(8,128)(2,1)S(1)}, bf16[1536,768]{1,0:T(8,128)(2,1)}, u32[]{:S(2)}) copy-start(bf16[1536,768]{1,0:T(8,128)(2,1)} %param.19) | copy-start | bytes 7077892
  100.9 34.3 %collective-permute-start.17 = (bf16[256,768]{1,0:T(8,128)(2,1)S(1)}, bf16[256,768]{1,0:T(8,128)(2,1)S(1)}, u32[]{:S(2)}, u32[]{:S(2)}) collective-permute-start(bf16[256,768]{1,0:T(8,128)(2,1)S(1)} %copy-done.15), channel_id=1, source_target_pairs={{0,2},{2,4},{4,6},{6,8},{8,10},{10,12},{12,14},{14,16},{16,18},{18... | collective-permute-start | bytes 1179656 | tf_op jit(solution)/shard_map/ppermute | solution.py:23
  105.4 29.8 %copy-start.5 = (f32[256,768]{1,0:T(8,128)S(1)}, f32[256,768]{1,0:T(8,128)}, u32[]{:S(2)}) copy-start(f32[256,768]{1,0:T(8,128)} %copy-done.4) | copy-start | bytes 2359300
  107.5 38.5 %collective-permute-start.12 = (bf16[384,1536]{1,0:T(8,128)(2,1)}, bf16[384,1536]{1,0:T(8,128)(2,1)}, u32[]{:S(2)}, u32[]{:S(2)}) collective-permute-start(bf16[384,1536]{1,0:T(8,128)(2,1)} %fusion.5), channel_id=1, source_target_pairs={{0,1},{1,0},{2,3},{3,2},{4,5},{5,4},{6,7},{7,6},{8,9},{9,8},{10,11... | collective-permute-start | bytes 3538952 | tf_op jit(solution)/shard_map/ppermute | solution.py:342
  145.7 13.4 %collective-permute-start.11 = (bf16[384,768]{1,0:T(8,128)(2,1)}, bf16[384,768]{1,0:T(8,128)(2,1)}, u32[]{:S(2)}, u32[]{:S(2)}) collective-permute-start(bf16[384,768]{1,0:T(8,128)(2,1)} %constant_dynamic-slice_fusion), channel_id=1, source_target_pairs={{0,1},{1,0},{2,3},{3,2},{4,5},{5,4},{6,7},{7,6},{8,9},{9,8},{10,11... | collective-permute-start | bytes 1769480 | tf_op jit(solution)/shard_map/ppermute | solution.py:352
  154.7 7.7 %collective-permute-start.13 = (bf16[384,768]{1,0:T(8,128)(2,1)S(1)}, bf16[384,768]{1,0:T(8,128)(2,1)S(1)}, u32[]{:S(2)}, u32[]{:S(2)}) collective-permute-start(bf16[384,768]{1,0:T(8,128)(2,1)S(1)} %constant_dynamic-slice_fusion.1), channel_id=1, source_target_pairs={{0,1},{1,0},{2,3},{3,2},{4,5},{5,4},{6,7},{7,6},{8,9},{9,8},{10,11... | collective-permute-start | bytes 1769480 | tf_op jit(solution)/shard_map/ppermute | solution.py:352
  160.4 9.0 %copy-start.6 = (bf16[31,768]{1,0:T(8,128)(2,1)S(1)}, bf16[31,768]{1,0:T(8,128)(2,1)}, u32[]{:S(2)}) copy-start(bf16[31,768]{1,0:T(8,128)(2,1)} %taps_ref.1) | copy-start | bytes 142852
  160.4 6.4 %collective-permute-start.15 = (bf16[16,768]{1,0:T(8,128)(2,1)S(1)}, bf16[16,768]{1,0:T(8,128)(2,1)S(1)}, u32[]{:S(2)}, u32[]{:S(2)}) collective-permute-start(bf16[16,768]{1,0:T(8,128)(2,1)S(1)} %slice.33), channel_id=1, source_target_pairs={{2,0},{4,2},{6,4},{8,6},{10,8},{12,10},{14,12},{16,14},{18,16},{20... | collective-permute-start | bytes 73736 | tf_op jit(solution)/shard_map/ppermute | solution.py:23
  162.8 6.6 %collective-permute-start.14 = (bf16[16,768]{1,0:T(8,128)(2,1)S(1)}, bf16[16,768]{1,0:T(8,128)(2,1)S(1)}, u32[]{:S(2)}, u32[]{:S(2)}) collective-permute-start(bf16[16,768]{1,0:T(8,128)(2,1)S(1)} %slice.32), channel_id=1, source_target_pairs={{0,2},{2,4},{4,6},{6,8},{8,10},{10,12},{12,14},{14,16},{16,18},{18... | collective-permute-start | bytes 73736 | tf_op jit(solution)/shard_map/ppermute | solution.py:23
  (13 other events, 18.7 us)

commit v2 on v1

--- a/solution.py
+++ b/solution.py
@@ -114,26 +114,275 @@
         frame_tiles(b_ref, bias_ref, offset, tile, body)
 
 
-def grads_kernel(offsets, tile, scale, n_stats, final, k_ref, v_ref, kt_ref, *refs):
+def bias_from(bounds_ref, bias_ref, tile):
+    frames, tokens = bias_ref.shape
+    begin, end = bounds_ref[0:1, :], bounds_ref[1:2, :]
+
+    def step(index, carry):
+        low = pl.multiple_of(index * tile, tile)
+        row = low + lax.broadcasted_iota(jnp.int32, (tile, tokens), 0)
+        inside = (row >= begin) & (row < end)
+        bias_ref[pl.ds(low, tile), :] = jnp.where(inside, 0.0, masked_fill)
+        return carry
+
+    lax.fori_loop(0, frames // tile, step, 0)
+
+
+def pair_stats(pair, tile, scale, k_ref, v_ref, q, u, bias_ref, out, qm_ref, um_ref):
+    frames, tokens = bias_ref.shape
+    _, _, window = qm_ref.shape
+    heads = out.shape[0] // 3
+    low = window_start(pair)
+    cols = slice(low, low + window)
+    column = lax.broadcasted_iota(jnp.int32, (1, window), 1)
+    for side in range(2):
+        at = (2 * pair + side) * HD - low
+        keep = jnp.where((column >= at) & (column < at + HD), 1.0, 0.0).astype(jnp.bfloat16)
+        qm_ref[side] = q[:, cols] * keep
+        um_ref[side] = u[:, cols] * keep
+
+    def step(index, carry):
+        rows = pl.ds(pl.multiple_of(index * tile, tile), tile)
+        keys, values = k_ref[rows, cols], v_ref[rows, cols]
+        bias = bias_ref[rows, :]
+        result = []
+        for side in range(2):
+            old, total, weighted = carry[3 * side : 3 * side + 3]
+            scores = contract_last(keys, qm_ref[side]) + bias
+            slopes = contract_last(values, um_ref[side])
+            new = jnp.maximum(old, jnp.max(scores, 0, keepdims=True))
+            fade = jnp.exp((old - new) * scale)
+            expos = jnp.exp((scores - new) * scale)
+            result += [
+                new,
+                total * fade + jnp.sum(expos, 0, keepdims=True),
+                weighted * fade + jnp.sum(expos * slopes, 0, keepdims=True),
+            ]
+        return tuple(result)
+
+    zero = jnp.zeros((1, tokens), jnp.float32)
+    start = (zero + masked_fill, zero, zero)
+    done = lax.fori_loop(0, frames // tile, step, start + start)
+    for side in range(2):
+        head = 2 * pair + side
+        for kind in range(3):
+            out[kind * heads + head : kind * heads + head + 1, :] = done[3 * side + kind]
+
+
+def exchange_kernel(
+    tile, scale, q_ref, u_ref, b_ref, k_ref, v_ref,
+    near, far, rel, own_ref, here_ref, peer_ref, back_ref,
+    transit, b_near, b_far, bias_ref, qm_ref, um_ref, send, recv_near, recv_y, recv_far,
+    stat_send, stat_recv, b_send, b_recv,
+):
+    me = lax.axis_index("tm")
+    count = lax.axis_size("tm")
+    frames = k_ref.shape[0]
+    heads = own_ref.shape[0] // 3
+    place = lax.rem(me, 4)
+    odd = lax.rem(me, 2)
+    x_peer = me + 1 - 2 * odd
+    y_peer = jnp.where(place < 2, me + 2, me - 2)
+    far_peer = me - 1 + 2 * odd
+    has_far = (far_peer >= 0) & (far_peer < count)
+    corner = (place == 0) | (place == 3)
+    up = jnp.where(place == 0, me + 4, me - 4)
+    down = jnp.where(place == 0, me - 4, me + 4)
+    has_up = corner & (up >= 0) & (up < count)
+    has_down = corner & (down >= 0) & (down < count)
+
+    barrier = pltpu.get_barrier_semaphore()
+
+    def greet(peer):
+        pl.semaphore_signal(
+            barrier, inc=1, device_id={"tm": peer}, device_id_type=pl.DeviceIdType.MESH
+        )
+
+    greet(x_peer)
+    greet(y_peer)
+    pl.when(has_far)(lambda: greet(far_peer))
+    pl.when(has_up)(lambda: greet(up))
+    pl.when(has_down)(lambda: greet(down))
+    callers = 2
+    for there in (has_far, has_up, has_down):
+        callers = callers + jnp.where(there, 1, 0)
+    pl.semaphore_wait(barrier, callers)
+
+    def remote(src, dst, send_sem, recv_sem, peer):
+        return pltpu.make_async_remote_copy(
+            src_ref=src, dst_ref=dst, send_sem=send_sem, recv_sem=recv_sem,
+            device_id={"tm": peer}, device_id_type=pl.DeviceIdType.MESH,
+        )
+
+    steps = 2 * (q_ref.shape[1] // LANES)
+
+    def part(c):
+        return slice((c // 2) * LANES, (c // 2 + 1) * LANES)
+
+    def first(c):
+        src = q_ref if c % 2 == 0 else u_ref
+        return remote(
+            src.at[:, part(c)], near.at[c % 2, :, part(c)], send.at[0, c], recv_near.at[c], x_peer
+        )
+
+    def second_final(c):
+        return remote(
+            near.at[c % 2, :, part(c)], far.at[c % 2, :, part(c)], send.at[1, c], recv_far.at[c], y_peer
+        )
+
+    def second_transit(c):
+        return remote(
+            near.at[c % 2, :, part(c)], transit.at[c % 2, :, part(c)], send.at[1, c], recv_y.at[c], y_peer
+        )
+
+    def third(c):
+        return remote(
+            transit.at[c % 2, :, part(c)], far.at[c % 2, :, part(c)], send.at[2, c], recv_far.at[c], up
+        )
+
+    to_near = remote(b_ref, b_near, b_send.at[0], b_recv.at[0], x_peer)
+    to_far = remote(b_ref, b_far, b_send.at[1], b_recv.at[1], far_peer)
+    to_near.start()
+    pl.when(has_far)(lambda: to_far.start())
+    for c in range(steps):
+        first(c).start()
+
+    @pl.when(jnp.logical_not(has_far))
+    def _():
+        far[...] = jnp.zeros_like(far)
+        b_far[...] = jnp.zeros_like(b_far)
+        peer_ref[1] = jnp.zeros_like(own_ref)
+        back_ref[1, 0:heads, :] = jnp.full((heads, own_ref.shape[1]), masked_fill, jnp.float32)
+        back_ref[1, heads:, :] = jnp.zeros((2 * heads, own_ref.shape[1]), jnp.float32)
+
+    base = me * frames
+    rel[0] = b_ref[...] - base
+    bias_from(rel.at[0], bias_ref.at[0], tile)
+
+    own_sends = [
+        remote(own_ref, peer_ref.at[0], stat_send.at[0], stat_recv.at[0], x_peer),
+        remote(own_ref, peer_ref.at[1], stat_send.at[1], stat_recv.at[1], far_peer),
+    ]
+    back_sends = [
+        remote(here_ref.at[0], back_ref.at[0], stat_send.at[2], stat_recv.at[2], x_peer),
+        remote(here_ref.at[1], back_ref.at[1], stat_send.at[3], stat_recv.at[3], far_peer),
+    ]
+
+    def own_unit(pair):
+        pair_stats(pair, tile, scale, k_ref, v_ref, q_ref, u_ref, bias_ref.at[0], own_ref, qm_ref, um_ref)
+        if pair == heads // 2 - 1:
+            own_sends[0].start()
+            pl.when(has_far)(lambda: own_sends[1].start())
+
+    def near_unit(pair):
+        pair_stats(
+            pair, tile, scale, k_ref, v_ref, near.at[0], near.at[1], bias_ref.at[1], here_ref.at[0], qm_ref, um_ref
+        )
+        if pair == heads // 2 - 1:
+            back_sends[0].start()
+
+    def far_unit(pair):
+        pair_stats(
+            pair, tile, scale, k_ref, v_ref, far.at[0], far.at[1], bias_ref.at[2], here_ref.at[1], qm_ref, um_ref
+        )
+
+    def need(pair):
+        return 2 * ((window_start(pair) + 2 * LANES) // LANES)
+
+    waited_far = [0]
+    passed_y = [0]
+
+    def pass_on(upto):
+        while passed_y[0] < upto:
+            c = passed_y[0]
+
+            @pl.when(corner)
+            def _():
+                second_transit(c).wait_recv()
+                pl.when(has_up)(lambda: third(c).start())
+
+            passed_y[0] += 1
+
+    def far_ready(upto):
+        while waited_far[0] < upto:
+            c = waited_far[0]
+            pl.when(has_far)(lambda: second_final(c).wait_recv())
+            waited_far[0] += 1
+
+    pairs = heads // 2
+    near_next, own_next, far_next = 0, 0, 0
+    for c in range(steps):
+        first(c).wait_recv()
+        pl.when(corner)(lambda: second_final(c).start())
+        pl.when(jnp.logical_not(corner))(lambda: second_transit(c).start())
+        pass_on(c - 1)
+        if c == 0:
+            to_near.wait_recv()
+            rel[1] = b_near[...] - base
+            bias_from(rel.at[1], bias_ref.at[1], tile)
+        if own_next < pairs:
+            own_unit(own_next)
+            own_next += 1
+        elif near_next < pairs and need(near_next) <= c + 1:
+            near_unit(near_next)
+            near_next += 1
+        elif far_next < pairs and need(far_next) <= c - 3:
+            if far_next == 0:
+                pl.when(has_far)(lambda: to_far.wait_recv())
+                rel[2] = b_far[...] - base
+                bias_from(rel.at[2], bias_ref.at[2], tile)
+            far_ready(need(far_next))
+            far_unit(far_next)
+            far_next += 1
+    while passed_y[0] < steps or near_next < pairs or far_next < pairs:
+        pass_on(min(steps, passed_y[0] + 1 if passed_y[0] < steps - 2 else steps))
+        if near_next < pairs:
+            near_unit(near_next)
+            near_next += 1
+            continue
+        if far_next < pairs:
+            if far_next == 0:
+                pl.when(has_far)(lambda: to_far.wait_recv())
+                rel[2] = b_far[...] - base
+                bias_from(rel.at[2], bias_ref.at[2], tile)
+            if need(far_next) > steps - 4:
+                pass_on(steps)
+            far_ready(need(far_next))
+            far_unit(far_next)
+            far_next += 1
+    far_ready(steps)
+    pl.when(has_far)(lambda: back_sends[1].start())
+
+    to_near.wait_send()
+    pl.when(has_far)(lambda: to_far.wait_send())
+    for c in range(steps):
+        first(c).wait_send()
+        second_final(c).wait_send()
+        pl.when(has_up)(lambda: third(c).wait_send())
+    own_sends[0].wait()
+    back_sends[0].wait()
+
+    @pl.when(has_far)
+    def _():
+        own_sends[1].wait()
+        back_sends[1].wait()
+
+
+def grads_kernel(offsets, n_stats, tile, scale, k_ref, v_ref, kt_ref, *refs):
     guests = len(offsets)
-    per = 3 + n_stats
-    inputs, refs = refs[: per * guests], refs[per * guests :]
-    if final:
-        dk_in, dv_in, dk_out, dv_out, dq_out = refs[:5]
-        dq_outs = [dq_out]
-        qm_ref, um_ref, bias_ref, norm_ref, dqt_ref, dk_ref, dv_ref = refs[5:]
-        dk_ref[...] = dk_in[...]
-        dv_ref[...] = dv_in[...]
-    else:
-        dk_ref, dv_ref = refs[:2]
-        dq_outs = refs[2 : 2 + guests]
-        qm_ref, um_ref, bias_ref, norm_ref, dqt_ref = refs[2 + guests :]
-        dk_ref[...] = jnp.zeros_like(dk_ref)
-        dv_ref[...] = jnp.zeros_like(dv_ref)
+    inputs = []
+    for kinds in n_stats:
+        inputs.append(refs[: 3 + kinds])
+        refs = refs[3 + kinds :]
+    dk_out, dv_out = refs[:2]
+    dq_outs = refs[2 : 2 + guests]
+    qm_ref, um_ref, bias_ref, norm_ref, dqt_ref, dk_ref, dv_ref = refs[2 + guests :]
+    dk_ref[...] = jnp.zeros_like(dk_ref)
+    dv_ref[...] = jnp.zeros_like(dv_ref)
     heads, tokens, window = qm_ref.shape
     for guest, offset in enumerate(offsets):
-        q_ref, u_ref, b_ref = inputs[per * guest : per * guest + 3]
-        stats = [r[...] for r in inputs[per * guest + 3 : per * guest + per]]
+        q_ref, u_ref, b_ref = inputs[guest][:3]
+        stats = [r[...] for r in inputs[guest][3:]]
         peak = stats[0][0:heads]
         for one in stats[1:]:
             peak = jnp.maximum(peak, one[0:heads])
@@ -179,9 +428,8 @@
 
         frame_tiles(b_ref, bias_ref, offset, tile, body)
         dq_outs[guest][...] = dqt_ref[...].T.astype(dq_outs[guest].dtype)
-    if final:
-        dk_out[...] = dk_ref[...].astype(jnp.bfloat16)
-        dv_out[...] = dv_ref[...].astype(jnp.bfloat16)
+    dk_out[...] = dk_ref[...].astype(jnp.bfloat16)
+    dv_out[...] = dv_ref[...].astype(jnp.bfloat16)
 
 
 def conv_kernel(block, h_ref, before_ref, after_ref, taps_ref, out_ref, x_ref, w_ref):
@@ -220,6 +468,11 @@
     return pltpu.CompilerParams(vmem_limit_bytes=None if mib is None else mib << 20)
 
 
+def relayed(tokens, width):
+    groups = lax.axis_size("tm") % 4 == 0
+    return groups and lax.axis_size("mp") == 2 and width % 384 == 0 and tokens % LANES == 0
+
+
 def attention(queries, upstream, bounds, frame_keys, frame_values):
     frames, width = frame_keys.shape
     tokens = queries.shape[0]
@@ -227,12 +480,7 @@
     window = window_of(width)
     scale = 1.0 / math.sqrt(HD)
     tile = tile_of(frames)
-    base = lax.axis_index("tm") * frames
-    local = (bounds - base).T
     f32, bf16 = jnp.float32, jnp.bfloat16
-    own = (queries, upstream, local)
-    prev = tuple(shifted(x, "tm", 1) for x in own)
-    after = tuple(shifted(x, "tm", -1) for x in own)
     keys_t = frame_keys.T
     shape = jax.ShapeDtypeStruct
     masks = [
@@ -242,66 +490,106 @@
     ]
     stat = shape((3 * heads, tokens), f32)
     work = 2 * tokens * frames * width
-
-    def stats(offsets, guests):
-        out = pl.pallas_call(
-            functools.partial(stats_kernel, offsets, tile, scale),
-            out_shape=[stat] * len(offsets),
-            in_specs=[VMEM] * (2 + 3 * len(offsets)),
-            out_specs=[VMEM] * len(offsets),
-            scratch_shapes=masks,
-            compiler_params=params(24),
+    peers = lax.axis_size("tm")
+
+    def grads(offsets, guests):
+        n_stats = tuple(len(guest) - 3 for guest in guests)
+        arrays = [x for guest in guests for x in guest]
+        return pl.pallas_call(
+            functools.partial(grads_kernel, offsets, n_stats, tile, scale),
+            out_shape=[shape((frames, width), bf16)] * 2
+            + [shape((tokens, width), bf16)] * 2
+            + [shape((tokens, width), f32)],
+            in_specs=[VMEM] * (3 + len(arrays)),
+            out_specs=[VMEM] * 5,
+            scratch_shapes=masks
+            + [pltpu.VMEM((2 * heads, tokens), f32), pltpu.VMEM((width, tokens), f32)]
+            + [pltpu.VMEM((frames, width), f32)] * 2,
+            compiler_params=params(40),
             cost_estimate=pl.CostEstimate(
-                flops=5 * work * len(offsets), bytes_accessed=4 * frames * width, transcendentals=0
+                flops=30 * work, bytes_accessed=20 * frames * width, transcendentals=0
             ),
-            name="stats%d" % len(offsets),
-        )(frame_keys, frame_values, *[x for guest in guests for x in guest])
-        return list(out)
-
-    (own_stats,) = stats((0,), (own,))
-    prev_own = shifted(own_stats, "tm", 1)
-    after_own = shifted(own_stats, "tm", -1)
-    prev_stats, after_stats = stats((-frames, frames), (prev, after))
-    from_after = shifted(prev_stats, "tm", -1)
-    from_prev = shifted(after_stats, "tm", 1)
-    position = lax.axis_index("tm")
-    last = lax.axis_size("tm") - 1
-    empty = jnp.where(jnp.arange(3 * heads) < heads, masked_fill, 0.0).astype(f32)[:, None]
-    from_prev = jnp.where(position == 0, empty, from_prev)
-    from_after = jnp.where(position == last, empty, from_after)
-
-    grad_scratch = [
-        pltpu.VMEM((2 * heads, tokens), f32),
-        pltpu.VMEM((width, tokens), f32),
-    ]
-    accs = [pltpu.VMEM((frames, width), f32)] * 2
-    dk, dv, prev_dq, after_dq = pl.pallas_call(
-        functools.partial(grads_kernel, (-frames, frames), tile, scale, 2, False),
-        out_shape=[shape((frames, width), f32)] * 2 + [shape((tokens, width), bf16)] * 2,
-        in_specs=[VMEM] * 13,
-        out_specs=[VMEM] * 4,
-        scratch_shapes=masks + grad_scratch,
-        compiler_params=params(32),
-        cost_estimate=pl.CostEstimate(
-            flops=20 * work, bytes_accessed=20 * frames * width, transcendentals=0
-        ),
-        name="grads2",
-    )(frame_keys, frame_values, keys_t, *prev, prev_stats, prev_own, *after, after_stats, after_own)
-    back_prev = shifted(prev_dq, "tm", -1)
-    back_after = shifted(after_dq, "tm", 1)
-    key_low, value_low, own_dq = pl.pallas_call(
-        functools.partial(grads_kernel, (0,), tile, scale, 3, True),
-        out_shape=[shape((frames, width), bf16)] * 2 + [shape((tokens, width), f32)],
-        in_specs=[VMEM] * 11,
-        out_specs=[VMEM] * 3,
-        scratch_shapes=masks + grad_scratch + accs,
-        compiler_params=params(40),
-        cost_estimate=pl.CostEstimate(
-            flops=10 * work, bytes_accessed=20 * frames * width, transcendentals=0
-        ),
-        name="grads1",
-    )(frame_keys, frame_values, keys_t, *own, own_stats, from_prev, from_after, dk, dv)
-    query_gradient = own_dq + back_prev.astype(f32) + back_after.astype(f32)
+            name="grads",
+        )(frame_keys, frame_values, keys_t, *arrays)
+
+    if relayed(tokens, width):
+        wide = shape((2, tokens, width), bf16)
+        steps = 2 * (width // LANES)
+        dma = pltpu.SemaphoreType.DMA
+        near, far, rel, own_stats, here, peer, back = pl.pallas_call(
+            functools.partial(exchange_kernel, tile, scale),
+            out_shape=[wide, wide, shape((3, 2, tokens), jnp.int32), stat]
+            + [shape((2, 3 * heads, tokens), f32)] * 3,
+            in_specs=[VMEM] * 5,
+            out_specs=[VMEM] * 7,
+            scratch_shapes=[
+                pltpu.VMEM((2, tokens, width), bf16),
+                pltpu.VMEM((2, tokens), jnp.int32),
+                pltpu.VMEM((2, tokens), jnp.int32),
+                pltpu.VMEM((3, frames, tokens), f32),
+                pltpu.VMEM((2, tokens, window), bf16),
+                pltpu.VMEM((2, tokens, window), bf16),
+                dma((3, steps)), dma((steps,)), dma((steps,)), dma((steps,)),
+                dma((4,)), dma((4,)), dma((2,)), dma((2,)),
+            ],
+            compiler_params=pltpu.CompilerParams(
+                collective_id=0, has_side_effects=True, vmem_limit_bytes=32 << 20
+            ),
+            name="exchange",
+        )(queries, upstream, bounds.T, frame_keys, frame_values)
+        key_low, value_low, near_dq, far_dq, own_dq = grads(
+            (0, 0, 0),
+            (
+                (near[0], near[1], rel[1], here[0], peer[0]),
+                (far[0], far[1], rel[2], here[1], peer[1]),
+                (queries, upstream, rel[0], own_stats, back[0], back[1]),
+            ),
+        )
+        terms = (
+            lax.ppermute(near_dq, "tm", [(i, i ^ 1) for i in range(peers)]),
+            lax.ppermute(
+                far_dq,
+                "tm",
+                [(i, i - 1 + 2 * (i % 2)) for i in range(peers) if 0 <= i - 1 + 2 * (i % 2) < peers],
+            ),
+        )
+    else:
+        base = lax.axis_index("tm") * frames
+        own = (queries, upstream, (bounds - base).T)
+        prev = tuple(shifted(x, "tm", 1) for x in own)
+        after = tuple(shifted(x, "tm", -1) for x in own)
+
+        def stats(offsets, guests):
+            return pl.pallas_call(
+                functools.partial(stats_kernel, offsets, tile, scale),
+                out_shape=[stat] * len(offsets),
+                in_specs=[VMEM] * (2 + 3 * len(offsets)),
+                out_specs=[VMEM] * len(offsets),
+                scratch_shapes=masks,
+                compiler_params=params(24),
+                name="stats%d" % len(offsets),
+            )(frame_keys, frame_values, *[x for guest in guests for x in guest])
+
+        (own_stats,) = stats((0,), (own,))
+        prev_own = shifted(own_stats, "tm", 1)
+        after_own = shifted(own_stats, "tm", -1)
+        prev_stats, after_stats = stats((-frames, frames), (prev, after))
+        from_after = shifted(prev_stats, "tm", -1)
+        from_prev = shifted(after_stats, "tm", 1)
+        position = lax.axis_index("tm")
+        empty = jnp.where(jnp.arange(3 * heads) < heads, masked_fill, 0.0).astype(f32)[:, None]
+        from_prev = jnp.where(position == 0, empty, from_prev)
+        from_after = jnp.where(position == peers - 1, empty, from_after)
+        key_low, value_low, prev_dq, after_dq, own_dq = grads(
+            (-frames, frames, 0),
+            (
+                (*prev, prev_stats, prev_own),
+                (*after, after_stats, after_own),
+                (*own, own_stats, from_prev, from_after),
+            ),
+        )
+        terms = (shifted(prev_dq, "tm", -1), shifted(after_dq, "tm", 1))
+    query_gradient = own_dq + terms[0].astype(f32) + terms[1].astype(f32)
     return key_low, value_low, query_gradient.astype(bf16)
 
 

time: 178 us -> 142 us (0.80)
  waiting for transfers between devices: 42.5 us -> 15.9 us
  starting transfers between devices: 44.9 us -> 19.7 us
  Pallas kernels: 45.7 us -> 65.4 us
    ppermute x14 -> x2, waiting for transfers between devices: 42.5 us -> 2.77 us  [shifted(): return lax.ppermute(value, axis, pairs)]
    ppermute x14 -> x2, starting transfers between devices: 44.5 us -> 5.97 us  [shifted(): return lax.ppermute(value, axis, pairs)]
    pallas_call x4 -> x2, Pallas kernels: 37.7 us -> 57.3 us  [the longest x1 31.7 us: attention(): pl.pallas_call(functools.partial(exchange_kernel, tile, scale), out_shape...]
    ppermute x0 -> x2, starting transfers between devices: none -> 13.4 us  [the longest x1 7 us: attention(): lax.ppermute(near_dq, 'tm', [(i, i ^ 1) for i in range(peers)])]
    ppermute x0 -> x2, waiting for transfers between devices: none -> 13.1 us  [the longest x1 8.71 us: attention(): lax.ppermute(near_dq, 'tm', [(i, i ^ 1) for i in range(peers)])]
    unnamed x55 -> x33, local copies, waits for them, and re-layouts: 9.85 us -> 8.57 us
  transfers between devices with their start and end apart: 18 -> 8, of which waited for: 5 -> 3; matrix products, arithmetic and copies ran while one was open for 18% -> 20% of each run, Pallas kernels for 15% -> 0%
where the time goes in v2:
time: 142 us; the launch traced here: 143 us
  Pallas kernels  65.4 us (46%)
  matrix products  23.8 us (17%)
  starting transfers between devices  19.7 us (14%)
  waiting for transfers between devices  15.9 us (11%)
  local copies, waits for them, and re-layouts  9.68 us (7%)
  other arithmetic  7.5 us (5%)
    pallas_call x1, Pallas kernels, attention(): pl.pallas_call(functools.partial(exchange_kernel, tile, scale), out_shape...  31.7 us
    pallas_call x1, Pallas kernels, grads(): pl.pallas_call(functools.partial(grads_kernel, offsets, n_stats, tile, sc...  25.6 us
    dot_general x6, matrix products, contract_last(): lax.dot_general(left, right, (((1,), (1,)), ((), ())), preferred_element_...  23.8 us
    ppermute x1, waiting for transfers between devices, attention(): lax.ppermute(near_dq, 'tm', [(i, i ^ 1) for i in range(peers)])  8.71 us
    unnamed x33, local copies, waits for them, and re-layouts  8.57 us
    pallas_call x1, Pallas kernels, depthwise(): pl.pallas_call(functools.partial(conv_kernel, tile_of(frames) // 4), out_...  8.01 us
    ppermute x1, starting transfers between devices, attention(): lax.ppermute(near_dq, 'tm', [(i, i ^ 1) for i in range(peers)])  7 us
    ppermute x1, starting transfers between devices, attention(): lax.ppermute(far_dq, 'tm', [(i, i - 1 + 2 * (i % 2)) for i in range(peers...  6.45 us
  transfers between devices with their start and end apart: 8, of which 3 were waited for; matrix products, arithmetic and copies ran while one was open for 20% of the time, Pallas kernels for 0%

profile of v2, /device:TPU:12, one launch (start us, length us, event | category | flops | bytes accessed | tf_op | source)
XLA Modules:
  0.0 142.9 jit_solution(14592190733595387559)
XLA Ops:
  0.7 2.5 %copy.13 = bf16[768,768]{0,1:T(8,128)(2,1)} copy(bf16[768,768]{1,0:T(8,128)(2,1)} %k_ref.3) | data formatting | bytes 2359296 | tf_op args[3]
  3.2 1.3 copy-done.3
  4.5 1.0 copy-done.7
  5.5 1.0 copy-done.9
  6.5 31.7 %exchange.1 = (bf16[2,256,768]{2,1,0:T(8,128)(2,1)S(1)}, bf16[2,256,768]{2,1,0:T(8,128)(2,1)S(1)}, s32[3,2,256]{2,1,0:T(2,128)S(1)}, f32[24,256]{1,0:T(8,128)S(1...) custom-call(bf16[256,768]{1,0:T(8,128)(2,1)S(1)} %copy-done.7, ...), custom_call_target="tpu_custom_call" | custom-call | tf_op jit(solution)/shard_map/exchange/pallas_call | solution.py:519
  38.4 1.1 copy-done.2
  39.4 0.4 copy-done.4
  39.9 0.1 copy-done.10
  40.0 25.6 %grads.1 = (bf16[768,768]{1,0:T(8,128)(2,1)S(1)}, bf16[768,768]{1,0:T(8,128)(2,1)S(1)}, bf16[256,768]{1,0:T(8,128)(2,1)}, bf16[256,768]{1,0:T(8,128)(2,1)}, f32[256,768]{1,0:T(8,128)S(1)}) custom-call(bf16[768,768]{1,0:T(8,128)(2,1)S(1)} %copy-done.1, bf16[768,768]{1,0:T(8,128)(2,1)S(1)} %copy-done.4, bf16[768,768]{1,0:T(8,128)(2,1)S(1)} %bitcast.36, ...), custom_call_target="tpu_custom_call" | custom-call | flops 9059696640 | bytes 11796480 | tf_op jit(solution)/shard_map/grads/pallas_call | solution.py:498
  65.6 1.1 fusion.26
  66.8 0.8 copy-done.15
  67.6 2.1 %fusion.4 = bf16[384,1536]{1,0:T(8,128)(2,1)} fusion(f32[384,1536]{1,0:T(8,128)S(1)} %fusion.26, bf16[1536,768]{1,0:T(8,128)(2,1)S(1)} %copy-done.15, bf16[768,768]{1,0:T(8,128)(2,1)S(1)} %get-tuple-element.22), kind=kOutput, calls=%fused_computation.14 | convolution fusion | flops 907149312 | bytes 6488064 | tf_op jit(solution)/shard_map/dot_general | solution.py:27
  69.7 7.0 %collective-permute-start.6 = (bf16[256,768]{1,0:T(8,128)(2,1)}, bf16[256,768]{1,0:T(8,128)(2,1)S(1)}, u32[]{:S(2)}, u32[]{:S(2)}) collective-permute-start(bf16[256,768]{1,0:T(8,128)(2,1)} %get-tuple-element.24), channel_id=1, source_target_pairs={{0,2},{2,0},{4,6},{6,4},{8,10},{10,8},{12,14},{14,12},{16,18},{18,... | collective-permute-start | bytes 1179656 | tf_op jit(solution)/shard_map/ppermute | solution.py:549
  76.7 6.4 %collective-permute-start.7 = (bf16[256,768]{1,0:T(8,128)(2,1)}, bf16[256,768]{1,0:T(8,128)(2,1)}, u32[]{:S(2)}, u32[]{:S(2)}) collective-permute-start(bf16[256,768]{1,0:T(8,128)(2,1)} %get-tuple-element.25), channel_id=1, source_target_pairs={{2,4},{4,2},{6,8},{8,6},{10,12},{12,10},{14,16},{16,14},{18,20},{2... | collective-permute-start | bytes 1179656 | tf_op jit(solution)/shard_map/ppermute | solution.py:550
  83.2 1.1 fusion.23
  84.3 2.1 %fusion.5 = bf16[384,1536]{1,0:T(8,128)(2,1)} fusion(f32[384,1536]{1,0:T(8,128)S(1)} %fusion.23, bf16[1536,768]{1,0:T(8,128)(2,1)S(1)} %copy-done.15, bf16[768,768]{1,0:T(8,128)(2,1)S(1)} %get-tuple-element.22), kind=kOutput, calls=%fused_computation.15 | convolution fusion | flops 907149312 | bytes 6488064 | tf_op jit(solution)/shard_map/dot_general | solution.py:27
  86.4 8.7 %collective-permute-done.6 = bf16[256,768]{1,0:T(8,128)(2,1)S(1)} collective-permute-done((bf16[256,768]{1,0:T(8,128)(2,1)}, bf16[256,768]{1,0:T(8,128)(2,1)S(1)}, u32[]{:S(2)}, u32[]{:S(2)}) %collective-permute-start.6) | collective-permute-done | bytes 393248 | tf_op jit(solution)/shard_map/ppermute | solution.py:549
  95.2 4.4 %collective-permute-done.7 = bf16[256,768]{1,0:T(8,128)(2,1)} collective-permute-done((bf16[256,768]{1,0:T(8,128)(2,1)}, bf16[256,768]{1,0:T(8,128)(2,1)}, u32[]{:S(2)}, u32[]{:S(2)}) %collective-permute-start.7) | collective-permute-done | bytes 393248 | tf_op jit(solution)/shard_map/ppermute | solution.py:550
  99.5 1.9 %add_convert_fusion.2 = bf16[256,768]{1,0:T(8,128)(2,1)} fusion(bf16[256,768]{1,0:T(8,128)(2,1)} %collective-permute-done.7, f32[256,768]{1,0:T(8,128)S(1)} %copy-done.6, bf16[256,768]{1,0:T(8,128)(2,1)S(1)} %collective-permute-done.6), kind=kLoop, calls=%fused_computation.33 | loop fusion | flops 983040 | bytes 1966080 | tf_op jit(solution)/shard_map/convert_element_type | solution.py:593
  101.4 8.7 %convolution_convert_fusion.1 = bf16[384,1536]{1,0:T(8,128)(2,1)S(1)} fusion(bf16[1536,1536]{1,0:T(8,128)(2,1)} %param.17, bf16[1536,1536]{1,0:T(8,128)(2,1)} %param.18, bf16[768,1536]{1,0:T(8,128)(2,1)} %param.16, bf16[384,1536]{1,0:T(8,128)(2,1)} %collective-permute-done, bf16[384,1536]{1,0:T(8,128)(2,1)} %fusion.4), kind=kOutput, calls=%fused_computation.11 | convolution fusion | flops 3633315840 | bytes 14155776 | tf_op jit(solution)/shard_map/dot_general | solution.py:27
  110.1 0.9 constant_dynamic-slice_fusion
  111.0 0.3 copy-done.13
  111.3 8.7 %convolution_convert_fusion = bf16[384,1536]{1,0:T(8,128)(2,1)S(1)} fusion(bf16[1536,1536]{1,0:T(8,128)(2,1)} %param.17, bf16[1536,1536]{1,0:T(8,128)(2,1)} %param.18, bf16[768,1536]{1,0:T(8,128)(2,1)} %param.16, bf16[384,1536]{1,0:T(8,128)(2,1)} %collective-permute-done.2, bf16[384,1536]{1,0:T(8,128)(2,1)} %fusion.5), kind=kOutput, calls=%fused_computation.10 | convolution fusion | flops 3633315840 | bytes 14155776 | tf_op jit(solution)/shard_map/dot_general | solution.py:27
  120.0 0.3 collective-permute-start.3
  120.3 2.0 %convert_add_fusion.1 = f32[384,1536]{1,0:T(8,128)S(1)} fusion(bf16[384,1536]{1,0:T(8,128)(2,1)} %collective-permute-done, bf16[384,1536]{1,0:T(8,128)(2,1)} %fusion.4), kind=kLoop, calls=%fused_computation.27 | loop fusion | flops 1769472 | bytes 4718592 | tf_op jit(solution)/shard_map/add | solution.py:631
  122.3 2.1 %convert_add_fusion = f32[384,1536]{1,0:T(8,128)S(1)} fusion(bf16[384,1536]{1,0:T(8,128)(2,1)} %collective-permute-done.2, bf16[384,1536]{1,0:T(8,128)(2,1)} %fusion.5), kind=kLoop, calls=%fused_computation.26 | loop fusion | flops 1769472 | bytes 4718592 | tf_op jit(solution)/shard_map/add | solution.py:631
  124.4 1.3 add_convert_fusion.1
  125.7 2.2 %collective-permute-start.5 = (bf16[16,768]{1,0:T(8,128)(2,1)S(1)}, bf16[16,768]{1,0:T(8,128)(2,1)S(1)}, u32[]{:S(2)}, u32[]{:S(2)}) collective-permute-start(bf16[16,768]{1,0:T(8,128)(2,1)S(1)} %slice.85), channel_id=1, source_target_pairs={{2,0},{4,2},{6,4},{8,6},{10,8},{12,10},{14,12},{16,14},{18,16},{20... | collective-permute-start | bytes 73736 | tf_op jit(solution)/shard_map/ppermute | solution.py:23
  128.0 0.3 add_convert_fusion
  128.2 3.8 %collective-permute-start.4 = (bf16[16,768]{1,0:T(8,128)(2,1)S(1)}, bf16[16,768]{1,0:T(8,128)(2,1)S(1)}, u32[]{:S(2)}, u32[]{:S(2)}) collective-permute-start(bf16[16,768]{1,0:T(8,128)(2,1)S(1)} %slice.84), channel_id=1, source_target_pairs={{0,2},{2,4},{4,6},{6,8},{8,10},{10,12},{12,14},{14,16},{16,18},{18... | collective-permute-start | bytes 73736 | tf_op jit(solution)/shard_map/ppermute | solution.py:23
  132.1 2.8 %collective-permute-done.4.before_ref = bf16[16,768]{1,0:T(8,128)(2,1)S(1)} collective-permute-done((bf16[16,768]{1,0:T(8,128)(2,1)S(1)}, bf16[16,768]{1,0:T(8,128)(2,1)S(1)}, u32[]{:S(2)}, u32[]{:S(2)}) %collective-permute-start.4) | collective-permute-done | bytes 24608 | tf_op jit(solution)/shard_map/ppermute | solution.py:23
  134.8 8.0 %conv.1 = bf16[768,768]{1,0:T(8,128)(2,1)} custom-call(bf16[768,768]{1,0:T(8,128)(2,1)S(1)} %pad_maximum_fusion.h_ref, bf16[16,768]{1,0:T(8,128)(2,1)S(1)} %collective-permute-done.4.before_ref, bf16[16,768]{1,0:T(8,128)(2,1)S(1)} %collective-permute-done.5.after_ref, bf16[31,768]{1,0:T(8,128)(2,1)S(1)} %copy-done.11), custom_call_target="tpu_custom_call" | custom-call | tf_op jit(solution)/shard_map/conv/pallas_call | solution.py:601
  (40 shorter events, 0.4 us)
Async XLA Ops:
  0.6 65.0 %copy-start = (bf16[1536,768]{1,0:T(8,128)(2,1)S(1)}, bf16[1536,768]{1,0:T(8,128)(2,1)}, u32[]{:S(2)}) copy-start(bf16[1536,768]{1,0:T(8,128)(2,1)} %param.19) | copy-start | bytes 7077892
  0.6 2.5 %copy-start.1 = (bf16[768,768]{1,0:T(8,128)(2,1)S(1)}, bf16[768,768]{1,0:T(8,128)(2,1)}, u32[]{:S(2)}) copy-start(bf16[768,768]{1,0:T(8,128)(2,1)} %k_ref.3) | copy-start | bytes 3538948
  0.7 2.5 %copy-start.12 = (s32[256,2]{0,1:T(2,128)S(1)}, s32[256,2]{0,1:T(2,128)}, u32[]{:S(2)}) copy-start(s32[256,2]{0,1:T(2,128)} %param.13) | copy-start | bytes 6148
  3.2 1.3 copy-start.3
  4.5 1.0 copy-start.7
  5.5 1.0 copy-start.9
  38.2 1.3 copy-start.2
  38.2 1.6 %copy-start.4 = (bf16[768,768]{1,0:T(8,128)(2,1)S(1)}, bf16[768,768]{1,0:T(8,128)(2,1)}, u32[]{:S(2)}) copy-start(bf16[768,768]{1,0:T(8,128)(2,1)} %v_ref.3) | copy-start | bytes 3538948
  38.2 1.7 %copy-start.8 = (bf16[256,768]{1,0:T(8,128)(2,1)S(1)}, bf16[256,768]{1,0:T(8,128)(2,1)}, u32[]{:S(2)}) copy-start(bf16[256,768]{1,0:T(8,128)(2,1)} %refs_10_.1) | copy-start | bytes 1179652
  38.2 1.8 %copy-start.10 = (bf16[256,768]{1,0:T(8,128)(2,1)S(1)}, bf16[256,768]{1,0:T(8,128)(2,1)}, u32[]{:S(2)}) copy-start(bf16[256,768]{1,0:T(8,128)(2,1)} %refs_11_.1) | copy-start | bytes 1179652
  65.6 1.1 copy-start.5
  65.6 1.9 %copy-start.15 = (bf16[1536,768]{1,0:T(8,128)(2,1)S(1)}, bf16[1536,768]{1,0:T(8,128)(2,1)}, u32[]{:S(2)}) copy-start(bf16[1536,768]{1,0:T(8,128)(2,1)} %param.20) | copy-start | bytes 7077892
  69.7 31.7 %collective-permute-start = (bf16[384,1536]{1,0:T(8,128)(2,1)}, bf16[384,1536]{1,0:T(8,128)(2,1)}, u32[]{:S(2)}, u32[]{:S(2)}) collective-permute-start(bf16[384,1536]{1,0:T(8,128)(2,1)} %fusion.4), channel_id=1, source_target_pairs={{0,1},{1,0},{2,3},{3,2},{4,5},{5,4},{6,7},{7,6},{8,9},{9,8},{10,11... | collective-permute-start | bytes 3538952 | tf_op jit(solution)/shard_map/ppermute | solution.py:630
  69.7 25.4 %collective-permute-start.6 = (bf16[256,768]{1,0:T(8,128)(2,1)}, bf16[256,768]{1,0:T(8,128)(2,1)S(1)}, u32[]{:S(2)}, u32[]{:S(2)}) collective-permute-start(bf16[256,768]{1,0:T(8,128)(2,1)} %get-tuple-element.24), channel_id=1, source_target_pairs={{0,2},{2,0},{4,6},{6,4},{8,10},{10,8},{12,14},{14,12},{16,18},{18,... | collective-permute-start | bytes 1179656 | tf_op jit(solution)/shard_map/ppermute | solution.py:549
  76.7 22.8 %collective-permute-start.7 = (bf16[256,768]{1,0:T(8,128)(2,1)}, bf16[256,768]{1,0:T(8,128)(2,1)}, u32[]{:S(2)}, u32[]{:S(2)}) collective-permute-start(bf16[256,768]{1,0:T(8,128)(2,1)} %get-tuple-element.25), channel_id=1, source_target_pairs={{2,4},{4,2},{6,8},{8,6},{10,12},{12,10},{14,16},{16,14},{18,20},{2... | collective-permute-start | bytes 1179656 | tf_op jit(solution)/shard_map/ppermute | solution.py:550
  84.3 15.2 %copy-start.6 = (f32[256,768]{1,0:T(8,128)S(1)}, f32[256,768]{1,0:T(8,128)}, u32[]{:S(2)}) copy-start(f32[256,768]{1,0:T(8,128)} %copy-done.5) | copy-start | bytes 2359300
  86.4 24.9 %collective-permute-start.2 = (bf16[384,1536]{1,0:T(8,128)(2,1)}, bf16[384,1536]{1,0:T(8,128)(2,1)}, u32[]{:S(2)}, u32[]{:S(2)}) collective-permute-start(bf16[384,1536]{1,0:T(8,128)(2,1)} %fusion.5), channel_id=1, source_target_pairs={{0,1},{1,0},{2,3},{3,2},{4,5},{5,4},{6,7},{7,6},{8,9},{9,8},{10,11... | collective-permute-start | bytes 3538952 | tf_op jit(solution)/shard_map/ppermute | solution.py:630
  110.1 1.2 copy-start.13
  111.0 13.4 %collective-permute-start.1 = (bf16[384,768]{1,0:T(8,128)(2,1)}, bf16[384,768]{1,0:T(8,128)(2,1)}, u32[]{:S(2)}, u32[]{:S(2)}) collective-permute-start(bf16[384,768]{1,0:T(8,128)(2,1)} %constant_dynamic-slice_fusion), channel_id=1, source_target_pairs={{0,1},{1,0},{2,3},{3,2},{4,5},{5,4},{6,7},{7,6},{8,9},{9,8},{10,11... | collective-permute-start | bytes 1769480 | tf_op jit(solution)/shard_map/ppermute | solution.py:640
  120.0 7.9 %collective-permute-start.3 = (bf16[384,768]{1,0:T(8,128)(2,1)S(1)}, bf16[384,768]{1,0:T(8,128)(2,1)S(1)}, u32[]{:S(2)}, u32[]{:S(2)}) collective-permute-start(bf16[384,768]{1,0:T(8,128)(2,1)S(1)} %constant_dynamic-slice_fusion.1), channel_id=1, source_target_pairs={{0,1},{1,0},{2,3},{3,2},{4,5},{5,4},{6,7},{7,6},{8,9},{9,8},{10,11... | collective-permute-start | bytes 1769480 | tf_op jit(solution)/shard_map/ppermute | solution.py:640
  122.3 2.1 %copy-start.14 = (bf16[384,1536]{1,0:T(8,128)(2,1)S(1)}, bf16[384,1536]{1,0:T(8,128)(2,1)}, u32[]{:S(2)}) copy-start(bf16[384,1536]{1,0:T(8,128)(2,1)} %copy-done.13) | copy-start | bytes 3538948
  125.7 9.1 %copy-start.11 = (bf16[31,768]{1,0:T(8,128)(2,1)S(1)}, bf16[31,768]{1,0:T(8,128)(2,1)}, u32[]{:S(2)}) copy-start(bf16[31,768]{1,0:T(8,128)(2,1)} %taps_ref.1) | copy-start | bytes 142852
  125.7 6.4 %collective-permute-start.5 = (bf16[16,768]{1,0:T(8,128)(2,1)S(1)}, bf16[16,768]{1,0:T(8,128)(2,1)S(1)}, u32[]{:S(2)}, u32[]{:S(2)}) collective-permute-start(bf16[16,768]{1,0:T(8,128)(2,1)S(1)} %slice.85), channel_id=1, source_target_pairs={{2,0},{4,2},{6,4},{8,6},{10,8},{12,10},{14,12},{16,14},{18,16},{20... | collective-permute-start | bytes 73736 | tf_op jit(solution)/shard_map/ppermute | solution.py:23
  128.2 6.6 %collective-permute-start.4 = (bf16[16,768]{1,0:T(8,128)(2,1)S(1)}, bf16[16,768]{1,0:T(8,128)(2,1)S(1)}, u32[]{:S(2)}, u32[]{:S(2)}) collective-permute-start(bf16[16,768]{1,0:T(8,128)(2,1)S(1)} %slice.84), channel_id=1, source_target_pairs={{0,2},{2,4},{4,6},{6,8},{8,10},{10,12},{12,14},{14,16},{16,18},{18... | collective-permute-start | bytes 73736 | tf_op jit(solution)/shard_map/ppermute | solution.py:23
